TPU v7x, 32 devices: a whole 2x2x4 slice. The times are simulated.
32 devices in a mesh: seq: 4 (over y, x), fsdp: 8 (over z, core).
Axes of the slice: x: 2, y: 2, z: 4, core: 2. Of those that a mesh axis runs over, the one named last changes fastest.
Arguments:
- tokens: bfloat16 [8, 1536, 1024], P('fsdp', 'seq'), may hold values from -6 to 6
- segment_ids: int32 [8, 1536], P('fsdp', 'seq'), may hold values from 0 to 5, never falling along the last dimension, each value on 1 to 768 neighbouring positions
- random_blocks: int32 [16, 22, 3], P('seq'), may hold values from 1 to 22, as said below
- ln1_gain: bfloat16 [1024], P('fsdp'), may hold values from 0.099609375 to 1.8984375
- ln1_bias: bfloat16 [1024], P('fsdp'), may hold values from -4 to 4
- w_qkv: bfloat16 [1024, 3072], P('fsdp'), may hold values from -0.25 to 0.25
- w_out: bfloat16 [1024, 1024], P('fsdp'), may hold values from -0.5 to 0.5
- ln2_gain: bfloat16 [1024], P('fsdp'), may hold values from 0.099609375 to 1.8984375
- ln2_bias: bfloat16 [1024], P('fsdp'), may hold values from -4 to 4
- w_in: bfloat16 [1024, 4096], P('fsdp'), may hold values from -0.1875 to 0.1875
- b_in: bfloat16 [4096], P('fsdp'), may hold values from -4 to 4
- w_down: bfloat16 [4096, 1024], P('fsdp'), may hold values from -0.09375 to 0.09375
- b_down: bfloat16 [1024], P('fsdp'), may hold values from -4 to 4
- cotangent: bfloat16 [8, 1536, 1024], P('fsdp', 'seq'), may hold values from -6 to 6
Outputs:
- output: bfloat16 [8, 1536, 1024], P('fsdp', 'seq')
- grad_tokens: bfloat16 [8, 1536, 1024], P('fsdp', 'seq')
- grad_ln1_gain: float32 [1024], P('fsdp')
- grad_ln1_bias: float32 [1024], P('fsdp')
- grad_qkv: float32 [1024, 3072], P('fsdp')
- grad_out_proj: float32 [1024, 1024], P('fsdp')
- grad_ln2_gain: float32 [1024], P('fsdp')
- grad_ln2_bias: float32 [1024], P('fsdp')
- grad_in: float32 [1024, 4096], P('fsdp')
- grad_in_bias: float32 [4096], P('fsdp')
- grad_down: float32 [4096, 1024], P('fsdp')
- grad_down_bias: float32 [1024], P('fsdp')
Inputs may be any that keep to these rules, and one draw needn't show every extreme that they name: For head h and query block b + 1, the 3 entries random_blocks[h, b, :] are different key blocks, none of them 0, 23, b, b + 1 or b + 2. `segment_ids`: in each sequence the segment numbers start at 0, never fall and take every value up to 5; a document has at most 768 tokens, and some document has exactly that many.
All inputs are finite; a program needn't handle non-finite values.
Results may differ from a plain program's by a relative error of at most 0.014.
Values may be sent and summed in bfloat16 or wider, within the bound.
A program may use at most 256 MiB of HBM per device.

v0:
```python
import functools
import math

import jax
import jax.numpy as jnp
from jax import lax
from jax.experimental import pallas as pl
from jax.experimental.pallas import tpu as pltpu
from jax.sharding import PartitionSpec as P

DH = 64
BLK = 64
LANES = 128
NEG = -1e30
F32 = jnp.float32
BF16 = jnp.bfloat16


def dot_nn(a, b):
    return jnp.dot(a, b, preferred_element_type=F32)


def dot_nt(a, b):
    return lax.dot_general(a, b, (((1,), (1,)), ((), ())), preferred_element_type=F32)


def dot_tn(a, b):
    return lax.dot_general(a, b, (((0,), (0,)), ((), ())), preferred_element_type=F32)


DOCS = 6


def block_mask(random_blocks):
    heads, inner, _ = random_blocks.shape
    blocks = inner + 2
    ids = jnp.arange(blocks, dtype=jnp.int32)
    near = jnp.abs(ids[:, None] - ids[None, :]) <= 1
    edge = (ids == 0) | (ids == blocks - 1)
    fixed = near | edge[:, None] | edge[None, :]
    picked = jnp.any(random_blocks[:, :, :, None] == ids, axis=2)
    used = fixed[None] | jnp.pad(picked, ((0, 0), (1, 1), (0, 0)))
    row = jnp.pad(jnp.where(used, 0.0, NEG), ((0, 0), (0, 0), (0, DH - blocks)))
    return jnp.concatenate([row, row], axis=-1)


def token_features(start, docs, blocks):
    shape = (docs.shape[0], LANES)
    lane = lax.rem(lax.broadcasted_iota(jnp.int32, shape, 1), DH)
    block = lax.div(lax.broadcasted_iota(jnp.int32, shape, 0) + start, BLK)
    own = docs + blocks == lane
    other = jnp.where(own | (lane >= blocks + DOCS), 0.0, 1.0)
    key_part = jnp.where(lane < blocks, jnp.where(block == lane, 1.0, 0.0), other)
    return jnp.where(own, NEG, 0.0).astype(BF16), key_part.astype(BF16)


def query_tile(q_tile, doc_tile, mask_ref, head, first_block, lanes):
    scale = jnp.asarray(1.0 / math.sqrt(DH), BF16)
    count = q_tile.shape[0] // BLK
    mask = jnp.concatenate(
        [jnp.broadcast_to(mask_ref[head, pl.ds(first_block + i, 1), :], (BLK, LANES)) for i in range(count)], axis=0
    )
    return jnp.where(lanes, q_tile * scale, doc_tile + mask.astype(BF16))


def own_lanes(odd, shape):
    return lax.div(lax.broadcasted_iota(jnp.int32, shape, 1), DH) == odd


MESH = pl.DeviceIdType.MESH


class Place:
    def __init__(self, fsdp_count):
        self.depth = fsdp_count // 2
        self.s = lax.axis_index("seq")
        self.f = lax.axis_index("fsdp")
        self.z = lax.div(self.f, 2)
        self.c = lax.rem(self.f, 2)
        self.s1 = self.s + 1 - 2 * lax.rem(self.s, 2)
        self.s2 = self.s + 2 - 4 * lax.div(self.s, 2)
        self.s3 = 3 - self.s
        self.beside = (self.s, self.f + 1 - 2 * self.c)

    def across(self, index):
        return ((self.s1, self.s2, self.s3)[index], self.f)

    def far(self, step):
        return lax.rem(self.z + step, self.depth)

    def back(self, step):
        return lax.rem(self.z + self.depth - step, self.depth)

    def along(self, z):
        return (self.s, 2 * z + self.c)

    def meet(self):
        barrier = pltpu.get_barrier_semaphore()
        peers = [self.beside] + [self.across(i) for i in range(3)]
        for peer in peers:
            pl.semaphore_signal(barrier, inc=1, device_id=peer, device_id_type=MESH)
        self.each(1, self.depth, lambda step: pl.semaphore_signal(
            barrier, inc=1, device_id=self.along(self.far(step)), device_id_type=MESH
        ))
        pl.semaphore_wait(barrier, len(peers) + self.depth - 1)

    def each(self, start, stop, body):
        if stop - start <= 8:
            for step in range(start, stop):
                body(step)
        else:
            lax.fori_loop(start, stop, lambda step, carry: (body(step), carry)[1], 0)


def send(src, dst, sems, index, device):
    sent, got = sems
    return pltpu.make_async_remote_copy(
        src_ref=src,
        dst_ref=dst,
        send_sem=sent.at[index],
        recv_sem=got.at[index],
        device_id=device,
        device_id_type=MESH,
    )


def aligned(start, size):
    return pl.ds(pl.multiple_of(start, size), size)


class Gather:
    def __init__(self, place, src, dst, split, sems):
        self.place, self.src, self.dst, self.split = place, src, dst, split
        self.rows, self.cols = src.shape
        self.local, self.zs, self.xs, self.rs, self.cs = sems

    def block(self, z, core, quarter=None, half=None):
        rows = aligned((2 * z + core) * self.rows, self.rows)
        if quarter is None:
            return self.dst.at[rows]
        wide = self.cols // 4
        if half is None:
            return self.dst.at[rows, aligned(quarter * wide, wide)]
        return self.dst.at[rows, aligned(quarter * wide + half * (wide // 2), wide // 2)]

    def source(self, step, side):
        return self.place.z - step if side == 0 else self.place.z + step

    def has(self, step, side):
        z = self.source(step, side)
        return z >= 0 if side == 0 else z < self.place.depth

    def sends(self, step, side):
        p = self.place
        onward = p.z + 1 < p.depth if side == 0 else p.z > 0
        return jnp.logical_and(self.has(step - 1, side), onward)

    def slot(self, step, side):
        return 2 * step + side

    def own_copy(self):
        return pltpu.make_async_copy(self.src, self.block(self.place.z, self.place.c), self.local)

    def own_core(self):
        p = self.place
        return send(self.src, self.block(p.z, p.c), self.cs, 0, p.beside)

    def own_arrival(self):
        p = self.place
        there = self.block(p.z, 1 - p.c)
        return send(there, there, self.cs, 0, p.beside)

    def core_copy(self, step, side):
        p = self.place
        there = self.block(self.source(step, side), p.c)
        return send(there, there, self.cs, self.slot(step, side), p.beside)

    def core_arrival(self, step, side):
        p = self.place
        there = self.block(self.source(step, side), 1 - p.c)
        return send(there, there, self.cs, self.slot(step, side), p.beside)

    def z_copy(self, step, side):
        p = self.place
        z = self.source(step - 1, side)
        there = self.block(z, p.c, p.s) if self.split else self.block(z, p.c)
        src = there
        if isinstance(step, int) and step == 1:
            wide = self.cols // 4
            src = self.src.at[:, aligned(p.s * wide, wide)] if self.split else self.src
        return send(src, there, self.zs, self.slot(step, side), p.along(p.z + 1 - 2 * side))

    def z_arrival(self, step, side):
        p = self.place
        z = self.source(step, side)
        there = self.block(z, p.c, p.s) if self.split else self.block(z, p.c)
        return send(there, there, self.zs, self.slot(step, side), p.along(p.z - 1 + 2 * side))

    def x_copy(self, step, side, way):
        p = self.place
        there = self.block(self.source(step, side), p.c, p.s)
        return send(there, there, self.xs[way], self.slot(step, side), p.across(way))

    def x_arrival(self, step, side, way):
        p = self.place
        there = self.block(self.source(step, side), p.c, (p.s1, p.s2)[way])
        return send(there, there, self.xs[way], self.slot(step, side), p.across(way))

    def relay_copy(self, step, side, way):
        p = self.place
        there = self.block(self.source(step, side), p.c, (p.s2, p.s1)[way], 1 - way)
        return send(there, there, self.rs[way], self.slot(step, side), p.across(way))

    def relay_arrival(self, step, side, way):
        p = self.place
        there = self.block(self.source(step, side), p.c, p.s3, 1 - way)
        return send(there, there, self.rs[way], self.slot(step, side), p.across(way))

    def both(self, step, body, test=None):
        for side in (0, 1):
            pl.when((test or self.has)(step, side))(functools.partial(body, step, side))

    def begin(self):
        self.both(1, lambda step, side: self.z_copy(step, side).start(), self.sends)
        self.own_copy().start()
        self.own_core().start()

    def swap(self, step):
        def body(step, side):
            self.z_arrival(step, side).wait_recv()
            pl.when(self.sends(step + 1, side))(lambda: self.z_copy(step + 1, side).start())
            if self.split:
                for way in (0, 1):
                    self.x_copy(step, side, way).start()
            else:
                self.core_copy(step, side).start()

        self.both(step, body)

    def relay(self, step):
        def body(step, side):
            for way in (0, 1):
                self.x_arrival(step, side, way).wait_recv()
            for way in (0, 1):
                self.relay_copy(step, side, way).start()

        if self.split:
            self.both(step, body)

    def share(self, step):
        def body(step, side):
            for way in (0, 1):
                self.relay_arrival(step, side, way).wait_recv()
            self.core_copy(step, side).start()

        if self.split:
            self.both(step, body)

    def finish(self):
        self.own_copy().wait()
        self.own_core().wait_send()
        self.own_arrival().wait_recv()

        def close(step, side):
            if self.split:
                for way in (0, 1):
                    self.x_copy(step, side, way).wait_send()
                    self.relay_copy(step, side, way).wait_send()
            self.core_copy(step, side).wait_send()
            self.core_arrival(step, side).wait_recv()

        self.place.each(1, self.place.depth, lambda step: self.both(step, close))
        self.place.each(
            1,
            self.place.depth,
            lambda step: self.both(step, lambda step, side: self.z_copy(step, side).wait_send(), self.sends),
        )

    @staticmethod
    def scratch(depth, split):
        held = 2 * depth if split else 1
        return [dma()] + [dma(2 * depth)] * 2 + [dma(held)] * 8 + [dma(2 * depth)] * 2

    @staticmethod
    def take(refs):
        pairs = [(refs[i], refs[i + 1]) for i in range(1, 13, 2)]
        return (refs[0], pairs[0], pairs[1:3], pairs[3:5], pairs[5])


GATHER_SEMS = 13


def gather_steps(place, gathers, late, count, unit):
    depth = place.depth

    def swap(step):
        for one in gathers:
            one.swap(step)

    def relay(step):
        for one in gathers:
            one.relay(step)

    def share(step):
        for one in gathers:
            one.share(step)

    def late_swap(step):
        for one in late:
            one.swap(step)

    for one in late:
        one.begin()
    if depth <= 8:
        rounds = []
        for step in range(2, depth + 2):
            now = []
            if step <= depth:
                now.append(functools.partial(late_swap, step - 2)) if step > 2 else None
                now.append(functools.partial(share, step - 3)) if step > 3 else None
                now.append(functools.partial(swap, step)) if step < depth else None
                now.append(functools.partial(relay, step - 1))
            rounds.append(now)
        rounds[-1] = [functools.partial(share, step) for step in range(max(1, depth - 2), depth)]
        rounds[-1].append(functools.partial(late_swap, depth - 1))
        in_turn(count, unit, rounds[:count])
        for now in rounds[count:]:
            for one in now:
                one()
    else:
        in_turn(count, unit, [])
        swap(2)
        relay(1)

        def body(step, carry):
            late_swap(step - 2)
            share(step - 2)
            swap(step)
            relay(step - 1)
            return carry

        lax.fori_loop(3, depth, body, 0)
        late_swap(depth - 2)
        share(depth - 2)
        relay(depth - 1)
        share(depth - 1)
        late_swap(depth - 1)


def dma(*shape):
    return pltpu.SemaphoreType.DMA(shape) if shape else pltpu.SemaphoreType.DMA


def qkv_columns(heads_ref, pair):
    third = heads_ref.shape[1] // 3
    return tuple(aligned(i * third + pair * LANES, LANES) for i in range(3))


def attend_unit(pair, odd, tile, heads_ref, mask_ref, qd_ref, kf_ref, keys_sc, values_t, out_ref, lse_ref):
    length = heads_ref.shape[0]
    cols = aligned(pair * LANES, LANES)
    q_cols, k_cols, v_cols = qkv_columns(heads_ref, pair)
    mine = own_lanes(odd, (length, LANES))
    keys_sc[...] = jnp.where(mine, heads_ref[:, k_cols], kf_ref[...])

    @pl.when(odd == 0)
    def _():
        values_t[...] = heads_ref[:, v_cols].T
        out_ref[:, cols] = jnp.zeros((length, LANES), BF16)

    def one_tile(index, carry):
        rows = aligned(index * tile, tile)
        lanes = own_lanes(odd, (tile, LANES))
        queries = query_tile(
            heads_ref[rows, q_cols], qd_ref[rows, :], mask_ref, 2 * pair + odd, index * (tile // BLK), lanes
        )
        scores = dot_nt(keys_sc[...], queries)
        top = jnp.max(scores, axis=0, keepdims=True)
        prob = jnp.exp(scores - top)
        total = jnp.sum(prob, axis=0, keepdims=True)
        mixed = dot_nn(values_t[...], prob.astype(BF16)) / total
        lse_ref[pair, pl.ds(odd, 1), rows] = top + jnp.log(total)
        out_ref[rows, cols] = jnp.where(lanes, mixed.T.astype(BF16), out_ref[rows, cols])
        return carry

    lax.fori_loop(0, length // tile, one_tile, 0, unroll=2)


def in_turn(count, unit, actions):
    def body(index, carry):
        unit(index)
        for which, todo in enumerate(actions):
            if todo:

                @pl.when(index == which)
                def _(todo=todo):
                    for one in todo:
                        one()

        return carry

    lax.fori_loop(0, count, body, 0)


def forward_kernel(
    fsdp_count,
    x_ref,
    wq_ref,
    vec_ref,
    seg_ref,
    mask_ref,
    out_w_ref,
    down_w_ref,
    in_w_ref,
    heads_all,
    lse_ref,
    att_all,
    out_w_all,
    down_w_all,
    in_w_all,
    vec_sum,
    n1_all,
    wq_all,
    qd_ref,
    kf_ref,
    x_sc,
    n1_sc,
    wq_own,
    wq_sc,
    vec_sc,
    seg_sc,
    heads_sc,
    att_sc,
    keys_sc,
    values_t,
    *sems,
):
    place = Place(fsdp_count)
    rows, width = x_ref.shape
    own_width = wq_sc.shape[1]
    seats = (place.s1, place.s2, place.s3)

    def taken(i):
        return Gather.take(sems[i * GATHER_SEMS : (i + 1) * GATHER_SEMS])

    x_own, seg_own, keep_sems, pick_sems, x_sent, x_got, r_sent, r_got, g_sent, g_got, a_sent, a_got, a_own = sems[6 * GATHER_SEMS :]
    lone = pl.ds(0, in_w_ref.shape[1] // 2)
    shared = pl.ds(in_w_ref.shape[1] // 2, in_w_ref.shape[1] // 2)
    gathers = [
        Gather(place, src, dst, split, taken(i))
        for i, (src, dst, split) in enumerate(
            (
                (out_w_ref, out_w_all, True),
                (in_w_ref.at[:, shared], in_w_all.at[:, shared], True),
                (down_w_ref, down_w_all, True),
                (in_w_ref.at[:, lone], in_w_all.at[:, lone], False),
            )
        )
    ]
    late = [gathers.pop()]
    third = own_width // 3
    picks = [
        pltpu.make_async_copy(
            wq_ref.at[:, aligned((4 * i + place.s) * third, third)], wq_own.at[:, pl.ds(i * third, third)], pick_sems.at[i]
        )
        for i in range(3)
    ]
    for pick in picks:
        pick.start()
    weight = Gather(place, wq_own, wq_sc, False, taken(4))
    vector = Gather(place, vec_ref, vec_sc, False, taken(5))
    half = rows // 2

    def x_rows(seat):
        return x_sc.at[aligned(seat * rows, rows)]

    def x_half(seat, part):
        return x_sc.at[aligned(seat * rows + part * half, half)]

    def x_copy(way):
        return send(x_ref, x_rows(place.s), (x_sent, x_got), way, place.across(way))

    def x_arrival(way):
        there = x_rows(seats[way])
        return send(there, there, (x_sent, x_got), way, place.across(way))

    def x_relay(way):
        there = x_half((place.s2, place.s1)[way], 1 - way)
        return send(there, there, (r_sent, r_got), way, place.across(way))

    def x_relayed(way):
        there = x_half(place.s3, 1 - way)
        return send(there, there, (r_sent, r_got), way, place.across(way))

    def seg_copy(way):
        return send(seg_ref, seg_sc.at[place.s], (g_sent, g_got), way, place.across(way))

    def seg_arrival(way):
        there = seg_sc.at[seats[way]]
        return send(there, there, (g_sent, g_got), way, place.across(way))

    place.meet()
    vector.begin()
    for pick in picks:
        pick.wait()
    weight.begin()
    for way in range(2):
        x_copy(way).start()
    for way in range(3):
        seg_copy(way).start()
    own_x = pltpu.make_async_copy(x_ref, x_rows(place.s), x_own)
    own_x.start()
    own_seg = pltpu.make_async_copy(seg_ref, seg_sc.at[place.s], seg_own)
    own_seg.start()
    def start_rest():
        for one in gathers:
            one.begin()

    if place.depth <= 8:
        for step in range(1, place.depth):
            vector.swap(step)
            weight.swap(step)
            if step == max(1, place.depth - 2):
                start_rest()
    else:
        place.each(1, place.depth, vector.swap)
        place.each(1, place.depth, weight.swap)
        start_rest()
    vector.finish()
    vec_rows = vec_ref.shape[0]
    total = vec_sc[pl.ds(0, vec_rows), :].astype(F32)
    if fsdp_count <= 8:
        for f in range(1, fsdp_count):
            total = total + vec_sc[pl.ds(f * vec_rows, vec_rows), :].astype(F32)
    else:
        total = lax.fori_loop(
            1, fsdp_count, lambda f, sofar: sofar + vec_sc[aligned(f * vec_rows, vec_rows), :].astype(F32), total
        )
    vec_sum[...] = total

    def normalise(seat):
        def body(part):
            token_rows = x_sc[aligned(seat * rows + part * 32, 32), :].astype(F32)
            center = token_rows - jnp.mean(token_rows, axis=-1, keepdims=True)
            variance = jnp.mean(center * center, axis=-1, keepdims=True)
            normed = center * lax.rsqrt(variance + 1e-05) * vec_sum[0:1, :] + vec_sum[1:2, :]
            n1_sc[aligned(seat * rows + part * 32, 32), :] = normed.astype(BF16)

        lax.fori_loop(0, rows // 32, lambda part, carry: (body(part), carry)[1], 0)

    def project(seat):
        here = aligned(seat * rows, rows)

        def body(part):
            cols = aligned(part * 256, 256)
            heads_sc[here, cols] = dot_nn(n1_sc[here, :], wq_sc[:, cols]).astype(BF16)

        lax.fori_loop(0, own_width // 256, lambda part, carry: (body(part), carry)[1], 0)

    own_x.wait()
    normalise(place.s)
    for way in range(2):
        x_arrival(way).wait_recv()
    for way in range(2):
        x_relay(way).start()
    for way in range(2):
        normalise(seats[way])
    weight.finish()
    project(place.s)
    for way in range(2):
        project(seats[way])
    for one in gathers:
        one.swap(1)
    for way in range(2):
        x_relayed(way).wait_recv()
    normalise(place.s3)
    project(place.s3)
    own_seg.wait()
    for way in range(3):
        seg_arrival(way).wait_recv()
    blocks = mask_ref.shape[1]
    for seat in range(4):
        columns = seg_sc[seat].T
        for part in range(rows // LANES):
            here = pl.ds(seat * rows + part * LANES, LANES)
            qd_ref[here, :], kf_ref[here, :] = token_features(
                seat * rows + part * LANES, columns[:, part : part + 1], blocks
            )
    keeps = [
        pltpu.make_async_copy(src, dst, keep_sems.at[i])
        for i, (src, dst) in enumerate(((heads_sc, heads_all), (n1_sc, n1_all), (wq_sc, wq_all)))
    ]
    for keep in keeps:
        keep.start()

    pairs = att_sc.shape[1] // LANES

    def att_copy(pair, way):
        cols = aligned((place.s * pairs + pair) * LANES, LANES)
        return send(
            att_sc.at[aligned(seats[way] * rows, rows), aligned(pair * LANES, LANES)],
            att_all.at[:, cols],
            (a_sent, a_got),
            pair * 3 + way,
            place.across(way),
        )

    def att_own(pair):
        cols = aligned((place.s * pairs + pair) * LANES, LANES)
        return pltpu.make_async_copy(
            att_sc.at[aligned(place.s * rows, rows), aligned(pair * LANES, LANES)],
            att_all.at[:, cols],
            a_own.at[pair],
        )

    def att_arrival(pair, way):
        there = att_all.at[:, aligned((seats[way] * pairs + pair) * LANES, LANES)]
        return send(there, there, (a_sent, a_got), pair * 3 + way, place.across(way))

    def unit(index):
        pair, odd = lax.div(index, 2), lax.rem(index, 2)
        attend_unit(pair, odd, 256, heads_sc, mask_ref, qd_ref, kf_ref, keys_sc, values_t, att_sc, lse_ref)

        @pl.when(odd == 1)
        def _():
            for way in range(3):
                att_copy(pair, way).start()
            att_own(pair).start()

    gather_steps(place, gathers, late, 2 * pairs, unit)
    for keep in keeps:
        keep.wait()
    for way in range(3):
        seg_copy(way).wait_send()
        if way < 2:
            x_copy(way).wait_send()
            x_relay(way).wait_send()
        for pair in range(pairs):
            att_copy(pair, way).wait_send()
            att_arrival(pair, way).wait_recv()
    for pair in range(pairs):
        att_own(pair).wait()
    for one in gathers + late:
        one.finish()


def forward_attention(fsdp_count, x, w_qkv, vec, seg, mask, w_out, w_down, w_in):
    rows, width = x.shape
    length = 4 * rows
    heads = mask.shape[0]
    pairs = heads // 2
    depth = fsdp_count // 2
    own_width = w_qkv.shape[1] // 4
    full = fsdp_count * w_qkv.shape[0]
    anywhere = pl.BlockSpec(memory_space=pltpu.HBM)
    vmem = pl.BlockSpec(memory_space=pltpu.VMEM)
    shape = jax.ShapeDtypeStruct

    def whole(shard):
        return shape((fsdp_count * shard.shape[0], shard.shape[1]), shard.dtype)

    return pl.pallas_call(
        functools.partial(forward_kernel, fsdp_count),
        out_shape=(
            shape((length, own_width), BF16),
            shape((pairs, 2, length), F32),
            shape((rows, heads * DH * 4), BF16),
            whole(w_out),
            whole(w_down),
            whole(w_in),
            shape(vec.shape, F32),
            shape((length, width), BF16),
            shape((full, own_width), BF16),
            shape((length, LANES), BF16),
            shape((length, LANES), BF16),
        ),
        in_specs=[anywhere] * 4 + [vmem] + [anywhere] * 3,
        out_specs=(anywhere, vmem, anywhere, anywhere, anywhere, anywhere, vmem, anywhere, anywhere, vmem, vmem),
        scratch_shapes=[
            pltpu.VMEM((length, width), BF16),
            pltpu.VMEM((length, width), BF16),
            pltpu.VMEM((w_qkv.shape[0], own_width), BF16),
            pltpu.VMEM((full, own_width), BF16),
            pltpu.VMEM((fsdp_count * vec.shape[0], vec.shape[1]), BF16),
            pltpu.VMEM((4,) + seg.shape, jnp.int32),
            pltpu.VMEM((length, own_width), BF16),
            pltpu.VMEM((length, heads * DH), BF16),
            pltpu.VMEM((length, LANES), BF16),
            pltpu.VMEM((LANES, length), BF16),
        ]
        + Gather.scratch(depth, True) * 3
        + Gather.scratch(depth, False) * 3
        + [dma(), dma(), dma(3), dma(3), dma(2), dma(2), dma(2), dma(2), dma(3), dma(3)]
        + [dma(3 * pairs), dma(3 * pairs), dma(pairs)],
        compiler_params=pltpu.CompilerParams(
            collective_id=2, has_side_effects=True, vmem_limit_bytes=60 << 20
        ),
    )(x, w_qkv, vec, seg, mask, w_out, w_down, w_in)


def by_rows(count, body):
    lax.fori_loop(0, count // 16, lambda i, carry: (body(aligned(i * 16, 16)), carry)[1], 0)


class Reduce:
    def __init__(self, place, grad, out, quartered, bufs, sems, direct=False, thirds=False, late=False, far_first=False):
        self.far_first = far_first
        self.place, self.grad, self.out, self.quartered, self.direct = place, grad, out, quartered, direct
        self.thirds, self.late = thirds, late
        self.rows, self.cols = out.shape
        self.wide = self.cols // 4
        self.acc, self.own, self.relay_in, self.quarter_in, self.z_in, self.total = bufs
        self.own_sem, self.put_sem, self.cs, self.rs, self.qs, self.zs, self.fs, self.gs = sems

    @staticmethod
    def scratch(depth, rows, cols, quartered, direct=False, far_first=False):
        held = cols // 4 if quartered else cols
        near = 1 if far_first else depth
        side = (1, 1, 16, LANES) if quartered else None
        return [
            pltpu.VMEM((depth, rows, held), BF16),
            pltpu.VMEM((16, LANES) if direct else (rows, held), BF16),
            pltpu.VMEM(side or (2, near, rows, cols // 8), BF16),
            pltpu.VMEM(side or (2, near, rows, cols // 4), BF16),
            pltpu.VMEM((depth, rows, cols if far_first else cols // 4), BF16),
            pltpu.VMEM((rows, cols // 4), BF16),
            dma(),
            dma(3),
        ] + [dma(depth)] * 12 + [dma(9)] * 2 + [dma(2)] * 2

    @staticmethod
    def take(place, grad, out, quartered, refs, direct=False, thirds=False, far_first=False):
        s = refs[8:]
        pairs = [(s[i], s[i + 1]) for i in range(0, 16, 2)]
        sems = (refs[6], refs[7], pairs[0], pairs[1:3], pairs[3:5], pairs[5], pairs[6], pairs[7])
        return Reduce(place, grad, out, quartered, refs[:6], sems, direct, thirds, False, far_first)

    def quarter(self, seat):
        return aligned(seat * self.wide, self.wide)

    def mine(self):
        if self.far_first:
            return pl.ds(0, self.cols)
        return pl.ds(0, self.wide) if self.quartered else self.quarter(self.place.s)

    def piece(self, seat, half):
        return aligned(seat * self.wide + half * (self.wide // 2), self.wide // 2)

    def own_copy(self, step):
        p = self.place
        rows = aligned((2 * p.far(step) + p.c) * self.rows, self.rows)
        return pltpu.make_async_copy(self.grad.at[rows], self.own, self.own_sem)

    def core_copy(self, step):
        p = self.place
        rows = aligned((2 * p.far(step) + 1 - p.c) * self.rows, self.rows)
        return send(self.grad.at[rows], self.acc.at[step], self.cs, step, p.beside)

    def relay_copy(self, step, way):
        p = self.place
        src = self.acc.at[step, :, self.piece(p.s3, way)]
        return send(src, self.relay_in.at[way, step], self.rs[way], step, p.across(way))

    def quarter_copy(self, step, way):
        p = self.place
        src = self.acc.at[step, :, self.quarter((p.s1, p.s2)[way])]
        return send(src, self.quarter_in.at[way, step], self.qs[way], step, p.across(way))

    def z_copy(self, step):
        p = self.place
        src = self.acc.at[step, :, self.mine()]
        return send(src, self.z_in.at[step], self.zs, step, p.along(p.far(step)))

    def columns(self, seat, part):
        if not self.thirds:
            return self.quarter(seat), pl.ds(0, self.wide)
        third = self.wide // 3
        return aligned((4 * part + seat) * third, third), pl.ds(part * third, third)

    @property
    def parts(self):
        return 3 if self.thirds else 1

    def put_copy(self, part):
        there, here = self.columns(self.place.s, part)
        return pltpu.make_async_copy(self.total.at[:, here], self.out.at[:, there], self.put_sem.at[part])

    def total_copy(self, way, part):
        p = self.place
        there, here = self.columns(p.s, part)
        return send(self.total.at[:, here], self.out.at[:, there], self.fs, 3 * way + part, p.across(way))

    def total_arrival(self, way, part):
        p = self.place
        there = self.out.at[:, self.columns((p.s1, p.s2, p.s3)[way], part)[0]]
        return send(there, there, self.fs, 3 * way + part, p.across(way))

    def totals(self):
        return [(way, part) for way in range(3 if self.thirds else 2) for part in range(self.parts)]

    def back_copy(self, way):
        p = self.place
        there = self.out.at[:, self.piece((p.s2, p.s1)[way], 1 - way)]
        return send(there, there, self.gs, way, p.across(way))

    def back_arrival(self, way):
        p = self.place
        there = self.out.at[:, self.piece(p.s3, 1 - way)]
        return send(there, there, self.gs, way, p.across(way))

    def begin(self):
        depth = self.place.depth
        self.place.each(1, depth, lambda step: self.core_copy(step).start())
        self.core_copy(0).start()
        self.own_copy(1).start()

    def fold(self, step, following):
        p, acc, own = self.place, self.acc, self.own
        self.core_copy(step).wait_recv()
        if not self.direct:
            self.own_copy(step).wait()
        base = (2 * p.far(step) + p.c) * self.rows

        def body(index, carry):
            rows = aligned(index * 16, 16)
            added = self.grad[aligned(base + index * 16, 16), :] if self.direct else own[rows, :]
            acc[step, rows, :] = acc[step, rows, :] + added
            return carry

        lax.fori_loop(0, self.rows // 16, body, 0)
        if following is not None:
            self.own_copy(following).start()
        if not (self.quartered or self.far_first):
            for way in (0, 1):
                self.relay_copy(step, way).start()
        elif not (isinstance(step, int) and step == 0):
            self.z_copy(step).start()

    def swap(self, step):
        if self.quartered:
            return
        p, acc = self.place, self.acc
        for way in (0, 1):
            self.relay_copy(step, way).wait_recv()
            cols = self.piece((p.s2, p.s1)[way], way)
            came = self.relay_in.at[way, step]

            def body(rows):
                acc[step, rows, cols] = acc[step, rows, cols] + came[rows, :]

            by_rows(self.rows, body)
        for way in (0, 1):
            self.quarter_copy(step, way).start()

    def close(self, step, own):
        if self.quartered:
            return
        p, acc, came = self.place, self.acc, self.quarter_in
        for way in (0, 1):
            self.quarter_copy(step, way).wait_recv()
        cols = self.quarter(p.s)

        def body(rows):
            acc[step, rows, cols] = (
                acc[step, rows, cols].astype(F32)
                + came[0, step, rows, :].astype(F32)
                + came[1, step, rows, :].astype(F32)
            ).astype(BF16)

        by_rows(self.rows, body)
        if not self.far_first:
            pl.when(jnp.logical_not(own))(lambda: self.z_copy(step).start())

    def far_sum(self):
        p, acc, came = self.place, self.acc, self.z_in
        p.each(1, p.depth, lambda step: self.z_copy(step).wait_recv())

        def body(rows):
            start = acc[0, rows, :].astype(F32)
            if p.depth <= 8:
                for step in range(1, p.depth):
                    start = start + came[step, rows, :].astype(F32)
            else:
                start = lax.fori_loop(1, p.depth, lambda step, sofar: sofar + came[step, rows, :].astype(F32), start)
            acc[0, rows, :] = start.astype(BF16)

        by_rows(self.rows, body)
        for way in (0, 1):
            self.relay_copy(0, way).start()

    def near_sum(self):
        self.close(0, True)
        total, acc, cols = self.total, self.acc, self.quarter(self.place.s)

        def body(rows):
            total[rows, :] = acc[0, rows, cols]

        by_rows(self.rows, body)
        self.give()

    def collect(self):
        p, acc, came, total = self.place, self.acc, self.z_in, self.total
        p.each(1, p.depth, lambda step: self.z_copy(step).wait_recv())
        cols = self.mine()

        def body(rows):
            start = acc[0, rows, cols].astype(F32)
            if p.depth <= 8:
                for step in range(1, p.depth):
                    start = start + came[step, rows, :].astype(F32)
            else:
                start = lax.fori_loop(1, p.depth, lambda step, sofar: sofar + came[step, rows, :].astype(F32), start)
            total[rows, :] = start.astype(BF16)

        by_rows(self.rows, body)
        if not self.direct:
            self.give()

    def give(self):
        for way, part in self.totals():
            self.total_copy(way, part).start()
        for part in range(self.parts):
            self.put_copy(part).start()

    def spread(self):
        for way, part in self.totals():
            self.total_arrival(way, part).wait_recv()
        if not self.thirds:
            for way in (0, 1):
                self.back_copy(way).start()

    def sent(self):
        def done(step):
            self.core_copy(step).wait_send()
            if not (self.quartered or self.far_first):
                for way in (0, 1):
                    self.relay_copy(step, way).wait_send()
                    self.quarter_copy(step, way).wait_send()

        self.place.each(0, self.place.depth, done)
        if self.far_first:
            for way in (0, 1):
                self.relay_copy(0, way).wait_send()
                self.quarter_copy(0, way).wait_send()

    def finish(self):
        for part in range(self.parts):
            self.put_copy(part).wait()
        if not self.late:
            self.sent()
            self.place.each(1, self.place.depth, lambda step: self.z_copy(step).wait_send())
        for way, part in self.totals():
            self.total_copy(way, part).wait_send()
        if not self.thirds:
            for way in (0, 1):
                self.back_arrival(way).wait_recv()
                self.back_copy(way).wait_send()


REDUCE_REFS = 24


def backward_unit(
    pair, odd, half, tile, heads_ref, mask_ref, qd_ref, kf_ref, go_ref, lse_ref, out_ref, keys_sc, values_sc, keys_t, p_sc, s_sc, k_acc, v_acc
):
    length = heads_ref.shape[0]
    span = p_sc.shape[1]
    scale = jnp.asarray(1.0 / math.sqrt(DH), BF16)
    q_cols, k_cols, v_cols = qkv_columns(heads_ref, pair)
    cols = aligned(pair * LANES, LANES)
    mine = own_lanes(odd, (length, LANES))

    @pl.when(half == 0)
    def _():
        keys_sc[...] = jnp.where(mine, heads_ref[:, k_cols], kf_ref[...])
        values_sc[...] = jnp.where(mine, heads_ref[:, v_cols], jnp.zeros((), BF16))
        keys_t[...] = heads_ref[:, k_cols].T
        k_acc[...] = jnp.zeros_like(k_acc)
        v_acc[...] = jnp.zeros_like(v_acc)

    def one_tile(index, carry):
        here = aligned(index * tile, tile)
        rows = aligned(half * span + index * tile, tile)
        lanes = own_lanes(odd, (tile, LANES))
        queries = query_tile(
            heads_ref[rows, q_cols],
            qd_ref[rows, :],
            mask_ref,
            2 * pair + odd,
            half * (span // BLK) + index * (tile // BLK),
            lanes,
        )
        prob = jnp.exp(dot_nt(keys_sc[...], queries) - lse_ref[pair, pl.ds(odd, 1), rows])
        grad_prob = dot_nt(values_sc[...], go_ref[rows, cols])
        delta = jnp.sum(prob * grad_prob, axis=0, keepdims=True)
        p_sc[:, here] = prob.astype(BF16)
        s_sc[:, here] = (prob * (grad_prob - delta)).astype(BF16)
        return carry

    lax.fori_loop(0, span // tile, one_tile, 0, unroll=True)
    part = aligned(half * span, span)
    v_acc[...] += dot_nn(p_sc[...], go_ref[part, cols])
    k_acc[...] += dot_nn(s_sc[...], heads_ref[part, q_cols] * scale)
    grad_q = (dot_nn(keys_t[...], s_sc[...]) * (1.0 / math.sqrt(DH))).T.astype(BF16)
    out_ref[part, q_cols] = jnp.where(own_lanes(odd, (span, LANES)), grad_q, out_ref[part, q_cols])

    @pl.when(half == 1)
    def _():
        out_ref[:, k_cols] = jnp.where(mine, k_acc[...].astype(BF16), out_ref[:, k_cols])
        out_ref[:, v_cols] = jnp.where(mine, v_acc[...].astype(BF16), out_ref[:, v_cols])


def backward_kernel(
    fsdp_count,
    go_hbm,
    heads_hbm,
    mask_ref,
    qd_hbm,
    kf_hbm,
    lse_ref,
    n1_ref,
    wq_hbm,
    x_hbm,
    hid_hbm,
    vec_ref,
    small_ref,
    out_g_ref,
    in_g_ref,
    down_part,
    tokens_out,
    small_out,
    qkv_total,
    out_total,
    in_total,
    down_total,
    go_sc,
    heads_ref,
    qd_ref,
    kf_ref,
    wq_ref,
    x_ref,
    hid_ref,
    load_sems,
    grads_sc,
    keys_sc,
    values_sc,
    keys_t,
    p_sc,
    s_sc,
    k_acc,
    v_acc,
    n1_sc,
    qkv_g,
    part_sc,
    part_in,
    half_in,
    small_sc,
    small_in,
    *rest,
):
    place = Place(fsdp_count)
    rows = x_ref.shape[0]
    cut_at = in_g_ref.shape[1] * 3 // 4
    shared = pl.ds(0, cut_at)
    apart = pl.ds(cut_at, in_g_ref.shape[1] - cut_at)
    reduces = [
        Reduce.take(place, grad, out, False, rest[i * REDUCE_REFS : (i + 1) * REDUCE_REFS])
        for i, (grad, out) in enumerate(
            ((out_g_ref, out_total), (in_g_ref.at[:, shared], in_total.at[:, shared]))
        )
    ]
    lone = Reduce.take(
        place,
        in_g_ref.at[:, apart],
        in_total.at[:, apart],
        False,
        rest[3 * REDUCE_REFS : 4 * REDUCE_REFS],
        far_first=True,
    )
    first = Reduce.take(place, qkv_g, qkv_total, True, rest[2 * REDUCE_REFS : 3 * REDUCE_REFS], thirds=True)
    put_sem, f_pair, g_pair = (
        rest[4 * REDUCE_REFS],
        rest[4 * REDUCE_REFS + 1 : 4 * REDUCE_REFS + 3],
        rest[4 * REDUCE_REFS + 3 : 4 * REDUCE_REFS + 5],
    )
    down = Reduce(
        place,
        None,
        down_total,
        True,
        (None, None, None, None, None, down_part),
        (None, put_sem, None, None, None, None, f_pair, g_pair),
        late=True,
    )
    n_own, h_sent, h_got, p_sent, p_got, c_sent, c_got, z_sent, z_got, x_sent, x_got = rest[
        4 * REDUCE_REFS + 5 :
    ]
    seats = (place.s1, place.s2, place.s3)
    width = go_sc.shape[1]
    pairs = width // LANES
    half = rows // 2

    loads = [
        pltpu.make_async_copy(src, dst, load_sems.at[i])
        for i, (src, dst) in enumerate(
            (
                (heads_hbm, heads_ref),
                (qd_hbm, qd_ref),
                (kf_hbm, kf_ref),
                (go_hbm, go_sc),
                (wq_hbm, wq_ref),
                (x_hbm, x_ref),
                (hid_hbm, hid_ref),
            )
        )
    ]
    for load in loads:
        load.start()
    later_loads = loads[4:]
    place.meet()
    for one in reduces:
        one.begin()
    lone.begin()
    down.give()
    n1_copy = pltpu.make_async_copy(n1_ref, n1_sc, n_own)
    n1_copy.start()

    def unit(index):
        backward_unit(
            lax.div(index, 4), lax.rem(lax.div(index, 2), 2), lax.rem(index, 2), 256, heads_ref, mask_ref, qd_ref, kf_ref,
            go_sc, lse_ref, grads_sc, keys_sc, values_sc, keys_t, p_sc, s_sc, k_acc, v_acc,
        )

    def half_copy(way):
        src = part_sc.at[aligned(place.s3 * rows + way * half, half)]
        return send(src, half_in.at[way], (h_sent, h_got), way, place.across(way))

    def part_copy(way, late):
        side = 1 - way if late else way
        src = part_sc.at[aligned(seats[way] * rows + side * half, half)]
        dst = part_in.at[way, pl.ds(side * half, half)]
        return send(src, dst, (p_sent, p_got), 2 * way + late, place.across(way))

    def partial_dn1():
        later_loads[0].wait()
        for seat in (place.s3, place.s1, place.s2, place.s):
            here = aligned(seat * rows, rows)
            part_sc[here, :] = dot_nt(grads_sc[here, :], wq_ref[...]).astype(BF16)
            for way in (0, 1):
                if seat is place.s3:
                    half_copy(way).start()
                elif seat is seats[way]:
                    part_copy(way, 0).start()

    def weight_grad():
        n1_copy.wait()

        def body(index):
            cols = aligned(index * 256, 256)
            qkv_g[cols, :] = dot_tn(n1_sc[:, cols], grads_sc[...]).astype(BF16)

        lax.fori_loop(0, qkv_g.shape[0] // 256, lambda index, carry: (body(index), carry)[1], 0)
        first.begin()

    def swap_dn1():
        for way in (0, 1):
            half_copy(way).wait_recv()
            base = (place.s2, place.s1)[way] * rows + way * half

            def body(index):
                here = aligned(base + index * 32, 32)
                came = half_in[way, aligned(index * 32, 32), :]
                part_sc[here, :] = (part_sc[here, :].astype(F32) + came.astype(F32)).astype(BF16)

            lax.fori_loop(0, half // 32, lambda index, carry: (body(index), carry)[1], 0)
        for way in (0, 1):
            part_copy(way, 1).start()

    def fold_first():
        depth = place.depth
        place.each(1, depth, lambda step: first.fold(step, lax.rem(step + 1, depth)))
        first.fold(0, None)

    def core_small():
        return send(small_sc.at[0], small_sc.at[1], (c_sent, c_got), 0, place.beside)

    def z_small(step):
        return send(small_sc.at[2], small_in.at[step], (z_sent, z_got), step, place.along(place.far(step)))

    def x_small(way):
        return send(small_sc.at[3], small_sc.at[4 + way], (x_sent, x_got), way, place.across(way))

    def close_dn1():
        for way in (0, 1):
            for late in (0, 1):
                part_copy(way, late).wait_recv()
        for load in later_loads[1:]:
            load.wait()
        gain = vec_ref[0:1, :]

        def body(index, sums):
            here = aligned(index * 32, 32)
            mine = aligned(place.s * rows + index * 32, 32)
            dn1 = (
                part_sc[mine, :].astype(F32)
                + part_in[0, here, :].astype(F32)
                + part_in[1, here, :].astype(F32)
            )
            token_rows = x_ref[here, :].astype(F32)
            center = token_rows - jnp.mean(token_rows, axis=-1, keepdims=True)
            inv = lax.rsqrt(jnp.mean(center * center, axis=-1, keepdims=True) + 1e-05)
            hat = center * inv
            scaled = dn1 * gain
            grad = hid_ref[here, :] + inv * (
                scaled
                - jnp.mean(scaled, axis=-1, keepdims=True)
                - hat * jnp.mean(scaled * hat, axis=-1, keepdims=True)
            )
            tokens_out[here, :] = grad.astype(BF16)
            return (
                sums[0] + jnp.sum(dn1 * hat, axis=0, keepdims=True),
                sums[1] + jnp.sum(dn1, axis=0, keepdims=True),
            )

        none = jnp.zeros((1, x_ref.shape[1]), F32)
        gain_sum, bias_sum = lax.fori_loop(0, rows // 32, body, (none, none))
        small_sc[0] = small_ref[...]
        small_sc[0, 0:1, :] = gain_sum
        small_sc[0, 1:2, :] = bias_sum
        core_small().start()

    def small_z():
        core_small().wait_recv()
        small_sc[2] = small_sc[0] + small_sc[1]
        place.each(1, place.depth, lambda step: z_small(step).start())

    def small_x():
        place.each(1, place.depth, lambda step: z_small(step).wait_recv())
        small_in[0] = small_sc[2]
        if place.depth <= 8:
            total = small_in[place.back(0)]
            for z in range(1, place.depth):
                total = total + small_in[place.back(z)]
        else:
            total = lax.fori_loop(
                1, place.depth, lambda z, sofar: sofar + small_in[place.back(z)], small_in[place.back(0)]
            )
        small_sc[3] = total
        for way in range(3):
            x_small(way).start()

    def small_end():
        for way in range(3):
            x_small(way).wait_recv()
        small_out[...] = (small_sc[3] + small_sc[4]) + (small_sc[5] + small_sc[6])

    depth = place.depth
    loose = depth > 8

    def run(count, body):
        lax.fori_loop(1, count, lambda step, carry: (body(step), carry)[1], 0)

    def fold(index):
        for one in [lone] + reduces:
            if not loose:
                step = (index + 1) % depth
                one.fold(step, (step + 1) % depth if step else None)
            elif index == 0:
                run(depth, lambda step: one.fold(step, lax.rem(step + 1, depth)))
                one.fold(0, None)

    def swap(index):
        for one in reduces:
            if not loose:
                one.swap((index + 1) % depth)
            elif index == 0:
                run(depth, one.swap)
                one.swap(0)

    def close(index):
        for one in reduces:
            if not loose:
                one.close((index + 1) % depth, (index + 1) % depth == 0)
            elif index == 0:
                run(depth, lambda step: one.close(step, False))
                one.close(0, True)

    rounds = 1 if loose else depth
    fold(0)
    if rounds > 1:
        fold(1)
    for load in loads[:4]:
        load.wait()
    steps = []
    for index in range(rounds + 2):
        if 2 <= index < rounds:
            steps.append(functools.partial(fold, index))
        if index < rounds:
            steps.append(functools.partial(swap, index))
        if 0 <= index - 1 < rounds:
            steps.append(functools.partial(close, index - 1))
    steps.insert(len(steps) // 2, down.spread)
    count = 4 * pairs
    grads_sc[...] = jnp.zeros_like(grads_sc)
    in_turn(count, unit, [steps[i * len(steps) // count : (i + 1) * len(steps) // count] for i in range(count)])
    partial_dn1()
    weight_grad()
    lone.far_sum()
    swap_dn1()
    lone.swap(0)
    for one in reduces:
        one.collect()
    fold_first()
    lone.near_sum()
    close_dn1()
    small_z()
    for one in reduces + [lone]:
        one.spread()
    first.collect()
    small_x()
    first.spread()
    small_end()
    core_small().wait_send()
    place.each(1, place.depth, lambda step: z_small(step).wait_send())
    for way in range(3):
        x_small(way).wait_send()
        if way < 2:
            half_copy(way).wait_send()
            for late in (0, 1):
                part_copy(way, late).wait_send()
    for one in [first, down, lone] + reduces:
        one.finish()


def backward_attention(fsdp_count, grad_heads, saved, x, hid, small, grads, down_part):
    heads, mask, qd, kf, lse, n1, wq, vec = saved
    rows, width = x.shape
    length, own_width = grad_heads.shape
    depth = fsdp_count // 2
    span = length // 2
    anywhere = pl.BlockSpec(memory_space=pltpu.HBM)
    vmem = pl.BlockSpec(memory_space=pltpu.VMEM)
    share = wq.shape[0] // fsdp_count
    kept = [(grad.shape[0] // fsdp_count, grad.shape[1]) for grad in grads]
    kept_qkv = (share, 4 * wq.shape[1])
    down_kept = (down_part.shape[0], 4 * down_part.shape[1])
    shape = jax.ShapeDtypeStruct

    reduce_scratch = []
    cut_at = kept[1][1] * 3 // 4
    for one in (kept[0], (kept[1][0], cut_at)):
        reduce_scratch += Reduce.scratch(depth, *one, False)
    reduce_scratch += Reduce.scratch(depth, *kept_qkv, True)
    reduce_scratch += Reduce.scratch(depth, kept[1][0], kept[1][1] - cut_at, False, far_first=True)
    return pl.pallas_call(
        functools.partial(backward_kernel, fsdp_count),
        out_shape=(shape(x.shape, BF16), shape(small.shape, F32), shape(kept_qkv, BF16))
        + tuple(shape(one, BF16) for one in kept)
        + (shape(down_kept, BF16),),
        in_specs=[anywhere] * 2 + [vmem] + [anywhere] * 2 + [vmem] + [anywhere] * 4 + [vmem] * 2 + [anywhere] * 2 + [vmem],
        out_specs=(vmem, vmem, anywhere, anywhere, anywhere, anywhere),
        scratch_shapes=[
            pltpu.VMEM((length, own_width), BF16),
            pltpu.VMEM(heads.shape, BF16),
            pltpu.VMEM(qd.shape, BF16),
            pltpu.VMEM(kf.shape, BF16),
            pltpu.VMEM(wq.shape, BF16),
            pltpu.VMEM(x.shape, BF16),
            pltpu.VMEM(hid.shape, F32),
            dma(7),
            pltpu.VMEM((length, 3 * own_width), BF16),
            pltpu.VMEM((length, LANES), BF16),
            pltpu.VMEM((length, LANES), BF16),
            pltpu.VMEM((LANES, length), BF16),
            pltpu.VMEM((length, span), BF16),
            pltpu.VMEM((length, span), BF16),
            pltpu.VMEM((length, LANES), F32),
            pltpu.VMEM((length, LANES), F32),
            pltpu.VMEM((length, width), BF16),
            pltpu.VMEM(wq.shape, BF16),
            pltpu.VMEM((length, width), BF16),
            pltpu.VMEM((2, rows, width), BF16),
            pltpu.VMEM((2, rows // 2, width), BF16),
            pltpu.VMEM((7,) + small.shape, F32),
            pltpu.VMEM((depth,) + small.shape, F32),
        ]
        + reduce_scratch
        + [dma(3), dma(9), dma(9), dma(2), dma(2)]
        + [dma(), dma(2), dma(2), dma(4), dma(4)]
        + [dma(1), dma(1), dma(depth), dma(depth), dma(3), dma(3)],
        compiler_params=pltpu.CompilerParams(
            collective_id=3, has_side_effects=True, vmem_limit_bytes=60 << 20
        ),
    )(grad_heads, heads, mask, qd, kf, lse, n1, wq, x, hid, vec, small, *grads, down_part)


def middle_kernel(
    fsdp_count,
    att_hbm,
    x_hbm,
    cot_hbm,
    vec_ref,
    out_w_hbm,
    in_w_ref,
    down_w_ref,
    result_ref,
    go_all,
    hid_ref,
    small_ref,
    out_g_ref,
    in_g_ref,
    down_part,
    att_ref,
    x_ref,
    cot_ref,
    out_w_ref,
    fetch_sems,
    datt_ref,
    go_sems,
    go_sent,
    go_got,
    hidden_sc,
    n2_sc,
    n2_t,
    out_acc,
    dn2_acc,
    in_buf,
    down_buf,
    grad_buf,
    down_g,
    in_sems,
    down_sems,
    grad_sems,
    *rest,
):
    place = Place(fsdp_count)
    depth = place.depth
    down_like = rest[0]
    total = Reduce.take(place, down_g, down_like, False, rest[1:], True)
    rows, width = x_ref.shape
    span = down_buf.shape[1]
    hidden_units = down_g.shape[0]
    chunks = hidden_units // span
    paired = total.rows == span
    lines = rows // 32

    def order(index):
        if not paired:
            return index
        z = place.far(lax.rem(lax.div(index, 2) + 1, depth))
        return 2 * z + jnp.where(lax.rem(index, 2) == 0, 1 - place.c, place.c)

    def in_load(index):
        slot = lax.rem(index, 2)
        return pltpu.make_async_copy(
            in_w_ref.at[:, aligned(order(index) * span, span)], in_buf.at[slot], in_sems.at[slot]
        )

    def down_load(index):
        slot = lax.rem(index, 2)
        return pltpu.make_async_copy(
            down_w_ref.at[aligned(order(index) * span, span)], down_buf.at[slot], down_sems.at[slot]
        )

    def grad_store(index):
        slot = lax.rem(index, 2)
        return pltpu.make_async_copy(
            grad_buf.at[slot], in_g_ref.at[:, aligned(order(index) * span, span)], grad_sems.at[slot]
        )

    def over_rows(body, start=0):
        return lax.fori_loop(0, lines, lambda index, carry: body(aligned(index * 32, 32), carry), start)

    in_load(0).start()
    down_load(0).start()
    loads = [
        pltpu.make_async_copy(src, dst, fetch_sems.at[i])
        for i, (src, dst) in enumerate(((att_hbm, att_ref), (out_w_hbm, out_w_ref), (x_hbm, x_ref), (cot_hbm, cot_ref)))
    ]
    for load in loads:
        load.start()
    place.meet()
    for load in loads:
        load.wait()
    hidden_sc[...] = x_ref[...].astype(F32) + dot_nn(att_ref[...], out_w_ref[...])

    def normalise(here, carry):
        token_rows = hidden_sc[here, :]
        center = token_rows - jnp.mean(token_rows, axis=-1, keepdims=True)
        variance = jnp.mean(center * center, axis=-1, keepdims=True)
        normed = center * lax.rsqrt(variance + 1e-05) * vec_ref[2:3, :] + vec_ref[3:4, :]
        n2_sc[here, :] = normed.astype(BF16)
        out_acc[here, :] = token_rows + vec_ref[4:5, :]
        return carry

    over_rows(normalise)
    n2_t[...] = n2_sc[...].T
    dn2_acc[...] = jnp.zeros_like(dn2_acc)
    small_ref[...] = jnp.zeros_like(small_ref)

    def chunk(index):
        slot = lax.rem(index, 2)
        which = order(index)
        in_load(index).wait()
        down_load(index).wait()

        def ahead():
            in_load(index + 1).start()
            down_load(index + 1).start()

        pl.when(index + 1 < chunks)(ahead)
        per = width // span
        line = pl.ds(5 + lax.div(which, per), 1)
        cols = aligned(lax.rem(which, per) * span, span)
        pre = dot_nn(n2_sc[...], in_buf[slot]) + vec_ref[line, cols]
        inner = jnp.tanh(0.7978845608028654 * (pre + 0.044715 * pre * pre * pre))
        act = (0.5 * pre * (1.0 + inner)).astype(BF16)
        slope = 0.5 * (1.0 + inner) + (0.5 * 0.7978845608028654) * pre * (1.0 - inner * inner) * (
            1.0 + (3.0 * 0.044715) * pre * pre
        )
        grad = dot_nt(cot_ref[...], down_buf[slot]) * slope
        low = grad.astype(BF16)
        small_ref[line, cols] = jnp.sum(low.astype(F32), axis=0, keepdims=True)
        down_g[aligned(which * span, span), :] = dot_tn(act, cot_ref[...]).astype(BF16)
        out_acc[...] += dot_nn(act, down_buf[slot])
        dn2_acc[...] += dot_nt(low, in_buf[slot])
        pl.when(index >= 2)(lambda: grad_store(index - 2).wait())
        grad_buf[slot] = dot_nn(n2_t[...], low).astype(BF16)
        grad_store(index).start()

    def later(t):
        pl.when(jnp.logical_and(t >= 1, t <= depth))(lambda: total.swap(lax.rem(t, depth)))
        pl.when(t >= 2)(lambda: total.close(lax.rem(t + depth - 1, depth), t == depth + 1))

    if paired:

        def step(t, carry):
            dest = lax.rem(t + 1, depth)

            def one(side, carry):
                chunk(2 * t + side)
                pl.when(side == 0)(lambda: total.core_copy(dest).start())
                return carry

            lax.fori_loop(0, 2, one, 0)
            total.fold(dest, None)
            later(t)
            return carry

        lax.fori_loop(0, depth, step, 0)
    else:
        lax.fori_loop(0, chunks, lambda index, carry: (chunk(index), carry)[1], 0)
        place.each(0, depth, lambda step: total.core_copy(step).start())

        def step(t, carry):
            total.fold(lax.rem(t + 1, depth), None)
            later(t)
            return carry

        lax.fori_loop(0, depth, step, 0)

    def finish(here, sums):
        token_rows = hidden_sc[here, :]
        center = token_rows - jnp.mean(token_rows, axis=-1, keepdims=True)
        inv = lax.rsqrt(jnp.mean(center * center, axis=-1, keepdims=True) + 1e-05)
        hat = center * inv
        dn2 = dn2_acc[here, :]
        cot = cot_ref[here, :].astype(F32)
        scaled = dn2 * vec_ref[2:3, :]
        grad = cot + inv * (
            scaled
            - jnp.mean(scaled, axis=-1, keepdims=True)
            - hat * jnp.mean(scaled * hat, axis=-1, keepdims=True)
        )
        hid_ref[here, :] = grad
        n2_sc[here, :] = grad.astype(BF16)
        result_ref[here, :] = out_acc[here, :].astype(BF16)
        return (
            sums[0] + jnp.sum(dn2 * hat, axis=0, keepdims=True),
            sums[1] + jnp.sum(dn2, axis=0, keepdims=True),
            sums[2] + jnp.sum(cot, axis=0, keepdims=True),
        )

    none = jnp.zeros((1, width), F32)
    gain_sum, bias_sum, cot_sum = over_rows(finish, (none, none, none))
    small_ref[2:3, :] = gain_sum
    small_ref[3:4, :] = bias_sum
    small_ref[4:5, :] = cot_sum
    later(depth)
    datt_ref[...] = dot_nt(n2_sc[...], out_w_ref[...]).astype(BF16)
    seats = (place.s1, place.s2, place.s3)
    part = width // 4

    def go_copy(way):
        src = datt_ref.at[:, aligned(seats[way] * part, part)]
        return send(src, go_all.at[aligned(place.s * rows, rows)], (go_sent, go_got), way, place.across(way))

    def go_arrival(way):
        there = go_all.at[aligned(seats[way] * rows, rows)]
        return send(there, there, (go_sent, go_got), way, place.across(way))

    own_go = pltpu.make_async_copy(
        datt_ref.at[:, aligned(place.s * part, part)], go_all.at[aligned(place.s * rows, rows)], go_sems
    )
    for way in range(3):
        go_copy(way).start()
    own_go.start()
    out_g_ref[...] = dot_tn(att_ref[...], n2_sc[...]).astype(BF16)
    later(depth + 1)
    total.collect()
    down_part[...] = total.total[...]
    for index in (chunks - 2, chunks - 1):
        grad_store(index).wait()
    own_go.wait()
    for way in range(3):
        go_arrival(way).wait_recv()
        go_copy(way).wait_send()
    total.sent()
    place.each(1, depth, lambda step: total.z_copy(step).wait_send())


def middle(fsdp_count, att, x, cot, vec, w_out, w_in, w_down):
    rows, width = x.shape
    hidden_units = w_in.shape[1]
    span = 512
    depth = fsdp_count // 2
    anywhere = pl.BlockSpec(memory_space=pltpu.HBM)
    vmem = pl.BlockSpec(memory_space=pltpu.VMEM)
    shape = jax.ShapeDtypeStruct
    kept = (hidden_units // fsdp_count, width)
    return pl.pallas_call(
        functools.partial(middle_kernel, fsdp_count),
        out_shape=(
            shape((rows, width), BF16),
            shape((4 * rows, width // 4), BF16),
            shape((rows, width), F32),
            shape(vec.shape, F32),
            shape(w_out.shape, BF16),
            shape(w_in.shape, BF16),
            shape((kept[0], width // 4), BF16),
        ),
        in_specs=[anywhere] * 3 + [vmem] + [anywhere] * 3,
        out_specs=(vmem, anywhere, vmem, vmem, vmem, anywhere, vmem),
        scratch_shapes=[
            pltpu.VMEM((rows, width), BF16),
            pltpu.VMEM((rows, width), BF16),
            pltpu.VMEM((rows, width), BF16),
            pltpu.VMEM(w_out.shape, BF16),
            dma(4),
            pltpu.VMEM((rows, width), BF16),
            dma(),
            dma(3),
            dma(3),
            pltpu.VMEM((rows, width), F32),
            pltpu.VMEM((rows, width), BF16),
            pltpu.VMEM((width, rows), BF16),
            pltpu.VMEM((rows, width), F32),
            pltpu.VMEM((rows, width), F32),
            pltpu.VMEM((2, width, span), BF16),
            pltpu.VMEM((2, span, width), BF16),
            pltpu.VMEM((2, width, span), BF16),
            pltpu.VMEM((hidden_units, width), BF16),
            dma(2),
            dma(2),
            dma(2),
            pltpu.VMEM(kept, BF16),
        ]
        + Reduce.scratch(depth, *kept, False, True),
        compiler_params=pltpu.CompilerParams(
            collective_id=5, has_side_effects=True, vmem_limit_bytes=60 << 20
        ),
    )(att, x, cot, vec, w_out, w_in, w_down)


def results_kernel(share, held, *refs):
    sources, small, refs = refs[:6], refs[6], refs[7:]
    cut = len(refs) > 20
    count = 12 if cut else 6
    outs, refs = refs[:count], refs[count:]
    taken, given, in_sems, out_sems = refs[:6], refs[6:12], refs[12], refs[13]
    loads = [pltpu.make_async_copy(src, dst, in_sems.at[i]) for i, (src, dst) in enumerate(zip(sources, taken))]
    for load in loads:
        load.start()
    stores = []
    for i, load in enumerate(loads):
        load.wait()
        src, dst = taken[i], given[i]
        chunk = 32 if src.shape[0] % 32 == 0 else 16

        def body(index, carry):
            rows = aligned(index * chunk, chunk)
            dst[rows, :] = src[rows, :].astype(dst.dtype)
            return carry

        if dst.dtype == src.dtype:
            store = pltpu.make_async_copy(src, outs[i], out_sems.at[i])
        else:
            lax.fori_loop(0, src.shape[0] // chunk, body, 0)
            store = pltpu.make_async_copy(dst, outs[i], out_sems.at[i])
        store.start()
        stores.append(store)
    if cut:
        position = lax.axis_index("fsdp")
        cols = aligned(position * share, share)
        for line in range(5):
            outs[6 + line][...] = small[line : line + 1, cols]
        per = small.shape[1] // held
        outs[11][...] = small[pl.ds(5 + lax.div(position, per), 1), aligned(lax.rem(position, per) * held, held)]
    for store in stores:
        store.wait()


def write_results(share, held, arrays, small):
    shape = jax.ShapeDtypeStruct
    kinds = (F32, F32, F32, F32, BF16, BF16)
    shapes = [shape(a.shape, kind) for a, kind in zip(arrays, kinds)]
    cut = share % LANES == 0 and held % LANES == 0
    small_shapes = [shape((1, share), F32)] * 5 + [shape((1, held), F32)] if cut else []
    hbm = pl.BlockSpec(memory_space=pltpu.HBM)
    vmem = pl.BlockSpec(memory_space=pltpu.VMEM)
    outs = pl.pallas_call(
        functools.partial(results_kernel, share, held),
        out_shape=tuple(shapes + small_shapes),
        in_specs=[hbm] * 6 + [vmem],
        out_specs=tuple([hbm] * 6 + [vmem] * len(small_shapes)),
        scratch_shapes=[pltpu.VMEM(a.shape, BF16) for a in arrays]
        + [pltpu.VMEM(a.shape if kind == F32 else (16, LANES), kind) for a, kind in zip(arrays, kinds)]
        + [dma(6), dma(6)],
        compiler_params=pltpu.CompilerParams(vmem_limit_bytes=60 << 20),
    )(*arrays, small)
    if cut:
        return outs[:6], [part.reshape(-1) for part in outs[6:]]
    position = lax.axis_index("fsdp")
    lines = lax.dynamic_slice_in_dim(small[:5], position * share, share, axis=1)
    rest = small[5:].reshape(-1)
    return outs, [lines[i] for i in range(5)] + [lax.dynamic_slice_in_dim(rest, position * held, held)]


def per_device(
    fsdp_count,
    tokens,
    segment_ids,
    random_blocks,
    ln1_gain,
    ln1_bias,
    w_qkv,
    w_out,
    ln2_gain,
    ln2_bias,
    w_in,
    b_in,
    w_down,
    b_down,
    cotangent,
):
    width = tokens.shape[2]
    share, held = ln1_gain.shape[0], b_in.shape[0]
    lines = fsdp_count * held // width
    position = lax.axis_index("fsdp")
    column = jnp.arange(width, dtype=jnp.int32)
    narrow = jnp.tile(jnp.stack([ln1_gain, ln1_bias, ln2_gain, ln2_bias, b_down]), (1, fsdp_count))
    narrow = jnp.where(column // share == position, narrow, jnp.zeros((), BF16))
    line = jnp.arange(lines, dtype=jnp.int32)[:, None]
    broad = jnp.tile(b_in[None], (1, width // held))
    broad = jnp.where((line * width + column) // held == position, broad, jnp.zeros((), BF16))
    vec = jnp.concatenate([narrow, broad, jnp.zeros((-(5 + lines) % 16, width), BF16)], axis=0)
    tok_count = segment_ids.shape[1]
    seg_rows = -(-tok_count // (8 * LANES)) * 8
    seg = jnp.pad(segment_ids[0], (0, seg_rows * LANES - tok_count)).reshape(seg_rows, LANES)
    mask = block_mask(random_blocks)
    by_heads, lse, att_rows, out_weight, down_weight, in_weight, vec, normed_one, own_qkv, query_docs, key_feats = (
        forward_attention(fsdp_count, tokens[0], w_qkv, vec, seg, mask, w_out, w_down, w_in)
    )
    result, grad_att, grad_hidden, small, grad_out, grad_in, down_part = middle(
        fsdp_count, att_rows, tokens[0], cotangent[0], vec, out_weight, in_weight, down_weight
    )
    grad_tokens, small, total_qkv, total_out, total_in, total_down = backward_attention(
        fsdp_count,
        grad_att,
        (by_heads, mask, query_docs, key_feats, lse, normed_one, own_qkv, vec),
        tokens[0],
        grad_hidden,
        small,
        (grad_out, grad_in),
        down_part,
    )
    arrays, parts = write_results(
        share, held, (total_in, total_down, total_qkv, total_out, result, grad_tokens), small
    )
    return (
        arrays[4][None],
        arrays[5][None],
        parts[0],
        parts[1],
        arrays[2],
        arrays[3],
        parts[2],
        parts[3],
        arrays[0],
        parts[5],
        arrays[1],
        parts[4],
    )


def solution(mesh):
    return jax.shard_map(
        functools.partial(per_device, mesh.shape["fsdp"]),
        mesh=mesh,
        in_specs=(
            P("fsdp", "seq", None),
            P("fsdp", "seq"),
            P("seq", None, None),
            P("fsdp"),
            P("fsdp"),
            P("fsdp", None),
            P("fsdp", None),
            P("fsdp"),
            P("fsdp"),
            P("fsdp", None),
            P("fsdp"),
            P("fsdp", None),
            P("fsdp"),
            P("fsdp", "seq", None),
        ),
        out_specs=(
            P("fsdp", "seq", None),
            P("fsdp", "seq", None),
            P("fsdp"),
            P("fsdp"),
            P("fsdp", None),
            P("fsdp", None),
            P("fsdp"),
            P("fsdp"),
            P("fsdp", None),
            P("fsdp"),
            P("fsdp", None),
            P("fsdp"),
        ),
        check_vma=False,
    )
```

profile of v0, /device:TPU:0, one launch (start us, length us, event | category | flops | bytes accessed | tf_op | source)
XLA Modules:
  0.0 284.2 jit_solution(2462102670760491065)
XLA Ops:
  0.6 0.0 copy-start
  0.7 0.1 pad.19.clone
  0.8 0.7 reduce
  1.5 0.6 pad_bitcast_fusion.seg_ref
  2.1 0.7 stack.23
  2.8 0.0 copy-done
  2.8 0.1 fusion.7
  2.9 0.1 fusion.5
  3.0 0.7 maximum_maximum_fusion.vec_ref
  3.7 0.8 copy.27
  4.5 0.2 fusion
  4.7 0.7 pad_maximum_fusion.mask_ref
  5.5 97.0 %shard_map.229 = (bf16[1536,768]{1,0:T(8,128)(2,1)}, f32[2,2,1536]{2,1,0:T(2,128)}, bf16[384,1024]{1,0:T(8,128)(2,1)}, bf16[1024,1024]{1,0:T(8,128)(2,1)}, bf16[...) custom-call(bf16[384,1024]{1,0:T(8,128)(2,1)} %bitcast.24, ...), custom_call_target="tpu_custom_call" | custom-call | tf_op jit(solution)/shard_map/pallas_call | solution.py:662
  102.5 67.2 %shard_map.230 = (bf16[384,1024]{1,0:T(8,128)(2,1)}, bf16[1536,256]{1,0:T(8,128)(2,1)}, f32[384,1024]{1,0:T(8,128)}, f32[16,1024]{1,0:T(8,128)}, bf16[1024,1024]...) custom-call(bf16[384,1024]{1,0:T(8,128)(2,1)} %get-tuple-element.48.att_hbm, ...), custom_call_target="tpu_custom_call" | custom-call | tf_op jit(solution)/shard_map/pallas_call | solution.py:1631
  169.6 108.4 %shard_map.231 = (bf16[384,1024]{1,0:T(8,128)(2,1)}, f32[16,1024]{1,0:T(8,128)}, bf16[128,3072]{1,0:T(8,128)(2,1)}, bf16[128,1024]{1,0:T(8,128)(2,1)}, bf16[128,...) custom-call(bf16[1536,256]{1,0:T(8,128)(2,1)} %get-tuple-element.53.go_hbm, bf16[1536,768]{1,0:T(8,128)(2,1)} %get-tuple-element.54.heads_hbm, ...), custom_call_target="tpu_custom_call" | custom-call | tf_op jit(solution)/shard_map/pallas_call | solution.py:1355
  278.0 6.0 %shard_map.232 = (f32[128,4096]{1,0:T(8,128)}, f32[512,1024]{1,0:T(8,128)}, f32[128,3072]{1,0:T(8,128)}, f32[128,1024]{1,0:T(8,128)}, bf16[384,1024]{1,0:T(8,128...) custom-call(bf16[128,4096]{1,0:T(8,128)(2,1)} %get-tuple-element.65., ...), custom_call_target="tpu_custom_call" | custom-call | tf_op jit(solution)/shard_map/pallas_call | solution.py:1721
  (11 shorter events, 0.1 us)
Async XLA Ops:
  0.6 2.2 copy-start
where the time goes:
time: 286 us; the launch traced here: 284 us
  Pallas kernels  279 us (98%)
    pallas_call x1, Pallas kernels, backward_attention(): pl.pallas_call(functools.partial(backward_kernel, fsdp_count), out_shape=...  108 us
    pallas_call x1, Pallas kernels, forward_attention(): pl.pallas_call(functools.partial(forward_kernel, fsdp_count), out_shape=(...  97 us
    pallas_call x1, Pallas kernels, middle(): pl.pallas_call(functools.partial(middle_kernel, fsdp_count), out_shape=(s...  67.2 us
    pallas_call x1, Pallas kernels, write_results(): pl.pallas_call(functools.partial(results_kernel, share, held), out_shape=...  6.04 us

commit v1 on v0

--- a/solution.py
+++ b/solution.py
@@ -407,7 +407,7 @@
     x_ref,
     wq_ref,
     vec_ref,
-    seg_ref,
+    ids_ref,
     mask_ref,
     out_w_ref,
     down_w_ref,
@@ -428,6 +428,7 @@
     wq_own,
     wq_sc,
     vec_sc,
+    seg_ref,
     seg_sc,
     heads_sc,
     att_sc,
@@ -467,6 +468,9 @@
     ]
     for pick in picks:
         pick.start()
+    seg_ref[...] = jnp.zeros_like(seg_ref)
+    for part in range(ids_ref.shape[1] // LANES):
+        seg_ref[part : part + 1, :] = ids_ref[:, part * LANES : (part + 1) * LANES]
     weight = Gather(place, wq_own, wq_sc, False, taken(4))
     vector = Gather(place, vec_ref, vec_sc, False, taken(5))
     half = rows // 2
@@ -652,6 +656,7 @@
     depth = fsdp_count // 2
     own_width = w_qkv.shape[1] // 4
     full = fsdp_count * w_qkv.shape[0]
+    seg_rows = -(-seg.shape[1] // (8 * LANES)) * 8
     anywhere = pl.BlockSpec(memory_space=pltpu.HBM)
     vmem = pl.BlockSpec(memory_space=pltpu.VMEM)
     shape = jax.ShapeDtypeStruct
@@ -674,7 +679,7 @@
             shape((length, LANES), BF16),
             shape((length, LANES), BF16),
         ),
-        in_specs=[anywhere] * 4 + [vmem] + [anywhere] * 3,
+        in_specs=[anywhere] * 3 + [vmem] * 2 + [anywhere] * 3,
         out_specs=(anywhere, vmem, anywhere, anywhere, anywhere, anywhere, vmem, anywhere, anywhere, vmem, vmem),
         scratch_shapes=[
             pltpu.VMEM((length, width), BF16),
@@ -682,7 +687,8 @@
             pltpu.VMEM((w_qkv.shape[0], own_width), BF16),
             pltpu.VMEM((full, own_width), BF16),
             pltpu.VMEM((fsdp_count * vec.shape[0], vec.shape[1]), BF16),
-            pltpu.VMEM((4,) + seg.shape, jnp.int32),
+            pltpu.VMEM((seg_rows, LANES), jnp.int32),
+            pltpu.VMEM((4, seg_rows, LANES), jnp.int32),
             pltpu.VMEM((length, own_width), BF16),
             pltpu.VMEM((length, heads * DH), BF16),
             pltpu.VMEM((length, LANES), BF16),
@@ -698,8 +704,11 @@
     )(x, w_qkv, vec, seg, mask, w_out, w_down, w_in)
 
 
-def by_rows(count, body):
-    lax.fori_loop(0, count // 16, lambda i, carry: (body(aligned(i * 16, 16)), carry)[1], 0)
+def by_rows(count, cols, body):
+    chunk = 16
+    while count % (2 * chunk) == 0 and 2 * chunk * cols <= 16384:
+        chunk *= 2
+    lax.fori_loop(0, count // chunk, lambda i, carry: (body(aligned(i * chunk, chunk)), carry)[1], 0)
 
 
 class Reduce:
@@ -848,7 +857,7 @@
             def body(rows):
                 acc[step, rows, cols] = acc[step, rows, cols] + came[rows, :]
 
-            by_rows(self.rows, body)
+            by_rows(self.rows, self.wide // 2, body)
         for way in (0, 1):
             self.quarter_copy(step, way).start()
 
@@ -867,7 +876,7 @@
                 + came[1, step, rows, :].astype(F32)
             ).astype(BF16)
 
-        by_rows(self.rows, body)
+        by_rows(self.rows, self.wide, body)
         if not self.far_first:
             pl.when(jnp.logical_not(own))(lambda: self.z_copy(step).start())
 
@@ -884,7 +893,7 @@
                 start = lax.fori_loop(1, p.depth, lambda step, sofar: sofar + came[step, rows, :].astype(F32), start)
             acc[0, rows, :] = start.astype(BF16)
 
-        by_rows(self.rows, body)
+        by_rows(self.rows, self.cols, body)
         for way in (0, 1):
             self.relay_copy(0, way).start()
 
@@ -895,7 +904,7 @@
         def body(rows):
             total[rows, :] = acc[0, rows, cols]
 
-        by_rows(self.rows, body)
+        by_rows(self.rows, self.wide, body)
         self.give()
 
     def collect(self):
@@ -912,7 +921,7 @@
                 start = lax.fori_loop(1, p.depth, lambda step, sofar: sofar + came[step, rows, :].astype(F32), start)
             total[rows, :] = start.astype(BF16)
 
-        by_rows(self.rows, body)
+        by_rows(self.rows, self.wide, body)
         if not self.direct:
             self.give()
 
@@ -1118,9 +1127,14 @@
         load.start()
     later_loads = loads[4:]
     place.meet()
-    for one in reduces:
-        one.begin()
-    lone.begin()
+    def first_copies(step):
+        for one in reduces + [lone]:
+            one.core_copy(step).start()
+
+    place.each(1, place.depth, first_copies)
+    first_copies(0)
+    for one in reduces + [lone]:
+        one.own_copy(1).start()
     down.give()
     n1_copy = pltpu.make_async_copy(n1_ref, n1_sc, n_own)
     n1_copy.start()
@@ -1261,7 +1275,7 @@
         lax.fori_loop(1, count, lambda step, carry: (body(step), carry)[1], 0)
 
     def fold(index):
-        for one in [lone] + reduces:
+        for one in reduces + [lone]:
             if not loose:
                 step = (index + 1) % depth
                 one.fold(step, (step + 1) % depth if step else None)
@@ -1427,6 +1441,8 @@
     in_buf,
     down_buf,
     grad_buf,
+    act_sc,
+    slope_sc,
     down_g,
     in_sems,
     down_sems,
@@ -1451,13 +1467,13 @@
         return 2 * z + jnp.where(lax.rem(index, 2) == 0, 1 - place.c, place.c)
 
     def in_load(index):
-        slot = lax.rem(index, 2)
+        slot = lax.rem(index, 4)
         return pltpu.make_async_copy(
             in_w_ref.at[:, aligned(order(index) * span, span)], in_buf.at[slot], in_sems.at[slot]
         )
 
     def down_load(index):
-        slot = lax.rem(index, 2)
+        slot = lax.rem(index, 4)
         return pltpu.make_async_copy(
             down_w_ref.at[aligned(order(index) * span, span)], down_buf.at[slot], down_sems.at[slot]
         )
@@ -1471,8 +1487,9 @@
     def over_rows(body, start=0):
         return lax.fori_loop(0, lines, lambda index, carry: body(aligned(index * 32, 32), carry), start)
 
-    in_load(0).start()
-    down_load(0).start()
+    for index in (0, 1):
+        in_load(index).start()
+        down_load(index).start()
     loads = [
         pltpu.make_async_copy(src, dst, fetch_sems.at[i])
         for i, (src, dst) in enumerate(((att_hbm, att_ref), (out_w_hbm, out_w_ref), (x_hbm, x_ref), (cot_hbm, cot_ref)))
@@ -1498,63 +1515,77 @@
     dn2_acc[...] = jnp.zeros_like(dn2_acc)
     small_ref[...] = jnp.zeros_like(small_ref)
 
-    def chunk(index):
-        slot = lax.rem(index, 2)
+    def place_of(which):
+        per = width // span
+        return pl.ds(5 + lax.div(which, per), 1), aligned(lax.rem(which, per) * span, span)
+
+    def activate(index):
+        slot, side = lax.rem(index, 4), lax.rem(index, 2)
         which = order(index)
         in_load(index).wait()
         down_load(index).wait()
 
         def ahead():
-            in_load(index + 1).start()
-            down_load(index + 1).start()
-
-        pl.when(index + 1 < chunks)(ahead)
-        per = width // span
-        line = pl.ds(5 + lax.div(which, per), 1)
-        cols = aligned(lax.rem(which, per) * span, span)
+            in_load(index + 2).start()
+            down_load(index + 2).start()
+
+        pl.when(index + 2 < chunks)(ahead)
+        line, cols = place_of(which)
         pre = dot_nn(n2_sc[...], in_buf[slot]) + vec_ref[line, cols]
         inner = jnp.tanh(0.7978845608028654 * (pre + 0.044715 * pre * pre * pre))
         act = (0.5 * pre * (1.0 + inner)).astype(BF16)
-        slope = 0.5 * (1.0 + inner) + (0.5 * 0.7978845608028654) * pre * (1.0 - inner * inner) * (
+        act_sc[side] = act
+        down_g[aligned(which * span, span), :] = dot_tn(act, cot_ref[...]).astype(BF16)
+        slope_sc[side] = 0.5 * (1.0 + inner) + (0.5 * 0.7978845608028654) * pre * (1.0 - inner * inner) * (
             1.0 + (3.0 * 0.044715) * pre * pre
         )
-        grad = dot_nt(cot_ref[...], down_buf[slot]) * slope
+
+    def chunk(index):
+        slot, side = lax.rem(index, 4), lax.rem(index, 2)
+        which = order(index)
+        line, cols = place_of(which)
+        grad = dot_nt(cot_ref[...], down_buf[slot]) * slope_sc[side]
         low = grad.astype(BF16)
         small_ref[line, cols] = jnp.sum(low.astype(F32), axis=0, keepdims=True)
-        down_g[aligned(which * span, span), :] = dot_tn(act, cot_ref[...]).astype(BF16)
-        out_acc[...] += dot_nn(act, down_buf[slot])
+        out_acc[...] += dot_nn(act_sc[side], down_buf[slot])
         dn2_acc[...] += dot_nt(low, in_buf[slot])
         pl.when(index >= 2)(lambda: grad_store(index - 2).wait())
-        grad_buf[slot] = dot_nn(n2_t[...], low).astype(BF16)
+        grad_buf[side] = dot_nn(n2_t[...], low).astype(BF16)
         grad_store(index).start()
 
-    def later(t):
-        pl.when(jnp.logical_and(t >= 1, t <= depth))(lambda: total.swap(lax.rem(t, depth)))
-        pl.when(t >= 2)(lambda: total.close(lax.rem(t + depth - 1, depth), t == depth + 1))
+    def swap_before(t):
+        pl.when(t >= 1)(lambda: total.swap(lax.rem(t, depth)))
+
+    def close_before(t):
+        pl.when(t >= 2)(lambda: total.close(lax.rem(t + depth - 1, depth), False))
 
     if paired:
 
         def step(t, carry):
             dest = lax.rem(t + 1, depth)
 
-            def one(side, carry):
-                chunk(2 * t + side)
+            def early(side, carry):
+                activate(2 * t + side)
                 pl.when(side == 0)(lambda: total.core_copy(dest).start())
                 return carry
 
-            lax.fori_loop(0, 2, one, 0)
+            lax.fori_loop(0, 2, early, 0)
+            swap_before(t)
+            chunk(2 * t)
             total.fold(dest, None)
-            later(t)
+            chunk(2 * t + 1)
+            close_before(t)
             return carry
 
         lax.fori_loop(0, depth, step, 0)
     else:
-        lax.fori_loop(0, chunks, lambda index, carry: (chunk(index), carry)[1], 0)
+        lax.fori_loop(0, chunks, lambda index, carry: (activate(index), chunk(index), carry)[2], 0)
         place.each(0, depth, lambda step: total.core_copy(step).start())
 
         def step(t, carry):
+            swap_before(t)
             total.fold(lax.rem(t + 1, depth), None)
-            later(t)
+            close_before(t)
             return carry
 
         lax.fori_loop(0, depth, step, 0)
@@ -1581,12 +1612,14 @@
             sums[2] + jnp.sum(cot, axis=0, keepdims=True),
         )
 
+    total.swap(0)
     none = jnp.zeros((1, width), F32)
     gain_sum, bias_sum, cot_sum = over_rows(finish, (none, none, none))
     small_ref[2:3, :] = gain_sum
     small_ref[3:4, :] = bias_sum
     small_ref[4:5, :] = cot_sum
-    later(depth)
+    if depth > 1:
+        total.close(depth - 1, False)
     datt_ref[...] = dot_nt(n2_sc[...], out_w_ref[...]).astype(BF16)
     seats = (place.s1, place.s2, place.s3)
     part = width // 4
@@ -1606,7 +1639,7 @@
         go_copy(way).start()
     own_go.start()
     out_g_ref[...] = dot_tn(att_ref[...], n2_sc[...]).astype(BF16)
-    later(depth + 1)
+    total.close(0, True)
     total.collect()
     down_part[...] = total.total[...]
     for index in (chunks - 2, chunks - 1):
@@ -1656,12 +1689,14 @@
             pltpu.VMEM((width, rows), BF16),
             pltpu.VMEM((rows, width), F32),
             pltpu.VMEM((rows, width), F32),
+            pltpu.VMEM((4, width, span), BF16),
+            pltpu.VMEM((4, span, width), BF16),
             pltpu.VMEM((2, width, span), BF16),
-            pltpu.VMEM((2, span, width), BF16),
-            pltpu.VMEM((2, width, span), BF16),
+            pltpu.VMEM((2, rows, span), BF16),
+            pltpu.VMEM((2, rows, span), F32),
             pltpu.VMEM((hidden_units, width), BF16),
-            dma(2),
-            dma(2),
+            dma(4),
+            dma(4),
             dma(2),
             pltpu.VMEM(kept, BF16),
         ]
@@ -1764,12 +1799,9 @@
     broad = jnp.tile(b_in[None], (1, width // held))
     broad = jnp.where((line * width + column) // held == position, broad, jnp.zeros((), BF16))
     vec = jnp.concatenate([narrow, broad, jnp.zeros((-(5 + lines) % 16, width), BF16)], axis=0)
-    tok_count = segment_ids.shape[1]
-    seg_rows = -(-tok_count // (8 * LANES)) * 8
-    seg = jnp.pad(segment_ids[0], (0, seg_rows * LANES - tok_count)).reshape(seg_rows, LANES)
     mask = block_mask(random_blocks)
     by_heads, lse, att_rows, out_weight, down_weight, in_weight, vec, normed_one, own_qkv, query_docs, key_feats = (
-        forward_attention(fsdp_count, tokens[0], w_qkv, vec, seg, mask, w_out, w_down, w_in)
+        forward_attention(fsdp_count, tokens[0], w_qkv, vec, segment_ids, mask, w_out, w_down, w_in)
     )
     result, grad_att, grad_hidden, small, grad_out, grad_in, down_part = middle(
         fsdp_count, att_rows, tokens[0], cotangent[0], vec, out_weight, in_weight, down_weight

time: 286 us -> 280 us (0.979)
  Pallas kernels: 279 us -> 275 us
    pallas_call x1, Pallas kernels: 108 us -> 104 us  [backward_attention(): pl.pallas_call(functools.partial(backward_kernel, fsdp_count), out_shape=...]
where the time goes in v1:
time: 280 us
  Pallas kernels  275 us (98%)
    pallas_call x1, Pallas kernels, backward_attention(): pl.pallas_call(functools.partial(backward_kernel, fsdp_count), out_shape=...  104 us
    pallas_call x1, Pallas kernels, forward_attention(): pl.pallas_call(functools.partial(forward_kernel, fsdp_count), out_shape=(...  97 us
    pallas_call x1, Pallas kernels, middle(): pl.pallas_call(functools.partial(middle_kernel, fsdp_count), out_shape=(s...  68.4 us
    pallas_call x1, Pallas kernels, write_results(): pl.pallas_call(functools.partial(results_kernel, share, held), out_shape=...  6.04 us

profile of v1, /device:TPU:0, one launch (start us, length us, event | category | flops | bytes accessed | tf_op | source)
XLA Modules:
  0.0 279.8 jit_solution(3208038642455788886)
XLA Ops:
  0.6 0.0 copy-start
  0.7 0.1 pad.14.clone
  0.8 0.7 stack.23
  1.5 0.0 copy-done
  1.5 0.1 fusion.7
  1.6 0.1 fusion.5
  1.7 0.7 maximum_maximum_fusion.vec_ref
  2.4 0.8 copy.27
  3.2 0.2 fusion
  3.5 0.7 pad_maximum_fusion.mask_ref
  4.2 97.0 %shard_map.229 = (bf16[1536,768]{1,0:T(8,128)(2,1)}, f32[2,2,1536]{2,1,0:T(2,128)}, bf16[384,1024]{1,0:T(8,128)(2,1)}, bf16[1024,1024]{1,0:T(8,128)(2,1)}, bf16[...) custom-call(bf16[384,1024]{1,0:T(8,128)(2,1)} %bitcast.22, ...), custom_call_target="tpu_custom_call" | custom-call | tf_op jit(solution)/shard_map/pallas_call | solution.py:667
  101.2 68.4 %shard_map.230 = (bf16[384,1024]{1,0:T(8,128)(2,1)}, bf16[1536,256]{1,0:T(8,128)(2,1)}, f32[384,1024]{1,0:T(8,128)}, f32[16,1024]{1,0:T(8,128)}, bf16[1024,1024]...) custom-call(bf16[384,1024]{1,0:T(8,128)(2,1)} %get-tuple-element.48.att_hbm, ...), custom_call_target="tpu_custom_call" | custom-call | tf_op jit(solution)/shard_map/pallas_call | solution.py:1664
  169.6 103.9 %shard_map.231 = (bf16[384,1024]{1,0:T(8,128)(2,1)}, f32[16,1024]{1,0:T(8,128)}, bf16[128,3072]{1,0:T(8,128)(2,1)}, bf16[128,1024]{1,0:T(8,128)(2,1)}, bf16[128,...) custom-call(bf16[1536,256]{1,0:T(8,128)(2,1)} %get-tuple-element.53.go_hbm, bf16[1536,768]{1,0:T(8,128)(2,1)} %get-tuple-element.54.heads_hbm, ...), custom_call_target="tpu_custom_call" | custom-call | tf_op jit(solution)/shard_map/pallas_call | solution.py:1369
  273.5 6.0 %shard_map.232 = (f32[128,4096]{1,0:T(8,128)}, f32[512,1024]{1,0:T(8,128)}, f32[128,3072]{1,0:T(8,128)}, f32[128,1024]{1,0:T(8,128)}, bf16[384,1024]{1,0:T(8,128...) custom-call(bf16[128,4096]{1,0:T(8,128)(2,1)} %get-tuple-element.65., ...), custom_call_target="tpu_custom_call" | custom-call | tf_op jit(solution)/shard_map/pallas_call | solution.py:1756
  (11 shorter events, 0.1 us)
Async XLA Ops:
  0.6 0.9 copy-start

commit v2 on v1

--- a/solution.py
+++ b/solution.py
@@ -1319,18 +1319,18 @@
     in_turn(count, unit, [steps[i * len(steps) // count : (i + 1) * len(steps) // count] for i in range(count)])
     partial_dn1()
     weight_grad()
+    swap_dn1()
+    fold_first()
     lone.far_sum()
-    swap_dn1()
-    lone.swap(0)
     for one in reduces:
         one.collect()
-    fold_first()
+    lone.swap(0)
+    first.collect()
+    close_dn1()
     lone.near_sum()
-    close_dn1()
     small_z()
     for one in reduces + [lone]:
         one.spread()
-    first.collect()
     small_x()
     first.spread()
     small_end()
@@ -1417,13 +1417,17 @@
     out_w_hbm,
     in_w_ref,
     down_w_ref,
-    result_ref,
+    result_hbm,
     go_all,
-    hid_ref,
+    hid_hbm,
     small_ref,
-    out_g_ref,
+    out_g_hbm,
     in_g_ref,
     down_part,
+    result_ref,
+    hid_ref,
+    out_g_ref,
+    put_sems,
     att_ref,
     x_ref,
     cot_ref,
@@ -1618,6 +1622,12 @@
     small_ref[2:3, :] = gain_sum
     small_ref[3:4, :] = bias_sum
     small_ref[4:5, :] = cot_sum
+    puts = [
+        pltpu.make_async_copy(src, dst, put_sems.at[i])
+        for i, (src, dst) in enumerate(((result_ref, result_hbm), (hid_ref, hid_hbm), (out_g_ref, out_g_hbm)))
+    ]
+    puts[0].start()
+    puts[1].start()
     if depth > 1:
         total.close(depth - 1, False)
     datt_ref[...] = dot_nt(n2_sc[...], out_w_ref[...]).astype(BF16)
@@ -1639,11 +1649,14 @@
         go_copy(way).start()
     own_go.start()
     out_g_ref[...] = dot_tn(att_ref[...], n2_sc[...]).astype(BF16)
+    puts[2].start()
     total.close(0, True)
     total.collect()
     down_part[...] = total.total[...]
     for index in (chunks - 2, chunks - 1):
         grad_store(index).wait()
+    for put in puts:
+        put.wait()
     own_go.wait()
     for way in range(3):
         go_arrival(way).wait_recv()
@@ -1673,8 +1686,12 @@
             shape((kept[0], width // 4), BF16),
         ),
         in_specs=[anywhere] * 3 + [vmem] + [anywhere] * 3,
-        out_specs=(vmem, anywhere, vmem, vmem, vmem, anywhere, vmem),
+        out_specs=(anywhere, anywhere, anywhere, vmem, anywhere, anywhere, vmem),
         scratch_shapes=[
+            pltpu.VMEM((rows, width), BF16),
+            pltpu.VMEM((rows, width), F32),
+            pltpu.VMEM(w_out.shape, BF16),
+            dma(3),
             pltpu.VMEM((rows, width), BF16),
             pltpu.VMEM((rows, width), BF16),
             pltpu.VMEM((rows, width), BF16),
@@ -1712,26 +1729,32 @@
     cut = len(refs) > 20
     count = 12 if cut else 6
     outs, refs = refs[:count], refs[count:]
-    taken, given, in_sems, out_sems = refs[:6], refs[6:12], refs[12], refs[13]
-    loads = [pltpu.make_async_copy(src, dst, in_sems.at[i]) for i, (src, dst) in enumerate(zip(sources, taken))]
+    taken, given, in_sems, out_sems = refs[:6], refs[6:10], refs[10], refs[11]
+    given = given + taken[4:]
+    pieces = []
+    for i in range(6):
+        rows = sources[i].shape[0]
+        parts = 4 if rows % 64 == 0 else 1
+        for part in range(parts):
+            pieces.append((i, part, pl.ds(part * (rows // parts), rows // parts), rows // parts))
+    loads = [
+        pltpu.make_async_copy(sources[i].at[here], taken[i].at[here], in_sems.at[i, part]) for i, part, here, _ in pieces
+    ]
     for load in loads:
         load.start()
     stores = []
-    for i, load in enumerate(loads):
+    for load, (i, part, here, rows) in zip(loads, pieces):
         load.wait()
-        src, dst = taken[i], given[i]
-        chunk = 32 if src.shape[0] % 32 == 0 else 16
+        src, dst, base = taken[i], given[i], part * rows
 
         def body(index, carry):
-            rows = aligned(index * chunk, chunk)
-            dst[rows, :] = src[rows, :].astype(dst.dtype)
+            line = aligned(base + index * 16, 16)
+            dst[line, :] = src[line, :].astype(F32)
             return carry
 
-        if dst.dtype == src.dtype:
-            store = pltpu.make_async_copy(src, outs[i], out_sems.at[i])
-        else:
-            lax.fori_loop(0, src.shape[0] // chunk, body, 0)
-            store = pltpu.make_async_copy(dst, outs[i], out_sems.at[i])
+        if i < 4:
+            lax.fori_loop(0, rows // 16, body, 0)
+        store = pltpu.make_async_copy(dst.at[here], outs[i].at[here], out_sems.at[i, part])
         store.start()
         stores.append(store)
     if cut:
@@ -1759,8 +1782,8 @@
         in_specs=[hbm] * 6 + [vmem],
         out_specs=tuple([hbm] * 6 + [vmem] * len(small_shapes)),
         scratch_shapes=[pltpu.VMEM(a.shape, BF16) for a in arrays]
-        + [pltpu.VMEM(a.shape if kind == F32 else (16, LANES), kind) for a, kind in zip(arrays, kinds)]
-        + [dma(6), dma(6)],
+        + [pltpu.VMEM(a.shape, F32) for a in arrays[:4]]
+        + [dma(6, 4), dma(6, 4)],
         compiler_params=pltpu.CompilerParams(vmem_limit_bytes=60 << 20),
     )(*arrays, small)
     if cut:

time: 280 us -> 278 us (level)
  no operation moved by 1% of the time
where the time goes in v2:
time: 278 us
  Pallas kernels  273 us (98%)
    pallas_call x1, Pallas kernels, backward_attention(): pl.pallas_call(functools.partial(backward_kernel, fsdp_count), out_shape=...  103 us
    pallas_call x1, Pallas kernels, forward_attention(): pl.pallas_call(functools.partial(forward_kernel, fsdp_count), out_shape=(...  97 us
    pallas_call x1, Pallas kernels, middle(): pl.pallas_call(functools.partial(middle_kernel, fsdp_count), out_shape=(s...  67 us
    pallas_call x1, Pallas kernels, write_results(): pl.pallas_call(functools.partial(results_kernel, share, held), out_shape=...  5.95 us

profile of v2, /device:TPU:0, one launch (start us, length us, event | category | flops | bytes accessed | tf_op | source)
XLA Modules:
  0.0 277.7 jit_solution(7427483810037148836)
XLA Ops:
  0.6 0.0 copy-start
  0.7 0.1 pad.14.clone
  0.8 0.7 stack.23
  1.5 0.0 copy-done
  1.5 0.1 fusion.7
  1.6 0.1 fusion.5
  1.7 0.7 maximum_maximum_fusion.vec_ref
  2.4 0.8 copy.27
  3.2 0.2 fusion
  3.5 0.7 pad_maximum_fusion.mask_ref
  4.2 97.0 %shard_map.229 = (bf16[1536,768]{1,0:T(8,128)(2,1)}, f32[2,2,1536]{2,1,0:T(2,128)}, bf16[384,1024]{1,0:T(8,128)(2,1)}, bf16[1024,1024]{1,0:T(8,128)(2,1)}, bf16[...) custom-call(bf16[384,1024]{1,0:T(8,128)(2,1)} %bitcast.22, ...), custom_call_target="tpu_custom_call" | custom-call | tf_op jit(solution)/shard_map/pallas_call | solution.py:667
  101.2 67.0 %shard_map.230 = (bf16[384,1024]{1,0:T(8,128)(2,1)}, bf16[1536,256]{1,0:T(8,128)(2,1)}, f32[384,1024]{1,0:T(8,128)}, f32[16,1024]{1,0:T(8,128)}, bf16[1024,1024]...) custom-call(bf16[384,1024]{1,0:T(8,128)(2,1)} %get-tuple-element.48.att_hbm, ...), custom_call_target="tpu_custom_call" | custom-call | tf_op jit(solution)/shard_map/pallas_call | solution.py:1677
  168.3 103.3 %shard_map.231 = (bf16[384,1024]{1,0:T(8,128)(2,1)}, f32[16,1024]{1,0:T(8,128)}, bf16[128,3072]{1,0:T(8,128)(2,1)}, bf16[128,1024]{1,0:T(8,128)(2,1)}, bf16[128,...) custom-call(bf16[1536,256]{1,0:T(8,128)(2,1)} %get-tuple-element.53.go_hbm, bf16[1536,768]{1,0:T(8,128)(2,1)} %get-tuple-element.54.heads_hbm, ...), custom_call_target="tpu_custom_call" | custom-call | tf_op jit(solution)/shard_map/pallas_call | solution.py:1369
  271.6 6.0 %shard_map.232 = (f32[128,4096]{1,0:T(8,128)}, f32[512,1024]{1,0:T(8,128)}, f32[128,3072]{1,0:T(8,128)}, f32[128,1024]{1,0:T(8,128)}, bf16[384,1024]{1,0:T(8,128...) custom-call(bf16[128,4096]{1,0:T(8,128)(2,1)} %get-tuple-element.65., ...), custom_call_target="tpu_custom_call" | custom-call | tf_op jit(solution)/shard_map/pallas_call | solution.py:1779
  (11 shorter events, 0.1 us)
Async XLA Ops:
  0.6 0.9 copy-start

commit v3 on v2

--- a/solution.py
+++ b/solution.py
@@ -735,7 +735,7 @@
             pltpu.VMEM((rows, cols // 4), BF16),
             dma(),
             dma(3),
-        ] + [dma(depth)] * 12 + [dma(9)] * 2 + [dma(2)] * 2
+        ] + [dma(depth)] * 12 + [dma(6)] * 4
 
     @staticmethod
     def take(place, grad, out, quartered, refs, direct=False, thirds=False, far_first=False):
@@ -805,17 +805,23 @@
         return send(there, there, self.fs, 3 * way + part, p.across(way))
 
     def totals(self):
-        return [(way, part) for way in range(3 if self.thirds else 2) for part in range(self.parts)]
-
-    def back_copy(self, way):
+        return [(way, part) for way in range(2) for part in range(self.parts)]
+
+    def split_piece(self, seat, part, half):
+        if not self.thirds:
+            return self.piece(seat, half)
+        width = self.wide // 6
+        return aligned(((4 * part + seat) * 2 + half) * width, width)
+
+    def back_copy(self, way, part):
         p = self.place
-        there = self.out.at[:, self.piece((p.s2, p.s1)[way], 1 - way)]
-        return send(there, there, self.gs, way, p.across(way))
-
-    def back_arrival(self, way):
+        there = self.out.at[:, self.split_piece((p.s2, p.s1)[way], part, 1 - way)]
+        return send(there, there, self.gs, 3 * way + part, p.across(way))
+
+    def back_arrival(self, way, part):
         p = self.place
-        there = self.out.at[:, self.piece(p.s3, 1 - way)]
-        return send(there, there, self.gs, way, p.across(way))
+        there = self.out.at[:, self.split_piece(p.s3, part, 1 - way)]
+        return send(there, there, self.gs, 3 * way + part, p.across(way))
 
     def begin(self):
         depth = self.place.depth
@@ -934,9 +940,8 @@
     def spread(self):
         for way, part in self.totals():
             self.total_arrival(way, part).wait_recv()
-        if not self.thirds:
-            for way in (0, 1):
-                self.back_copy(way).start()
+        for way, part in self.totals():
+            self.back_copy(way, part).start()
 
     def sent(self):
         def done(step):
@@ -960,10 +965,9 @@
             self.place.each(1, self.place.depth, lambda step: self.z_copy(step).wait_send())
         for way, part in self.totals():
             self.total_copy(way, part).wait_send()
-        if not self.thirds:
-            for way in (0, 1):
-                self.back_arrival(way).wait_recv()
-                self.back_copy(way).wait_send()
+        for way, part in self.totals():
+            self.back_arrival(way, part).wait_recv()
+            self.back_copy(way, part).wait_send()
 
 
 REDUCE_REFS = 24
@@ -1399,7 +1403,7 @@
             pltpu.VMEM((depth,) + small.shape, F32),
         ]
         + reduce_scratch
-        + [dma(3), dma(9), dma(9), dma(2), dma(2)]
+        + [dma(3), dma(6), dma(6), dma(6), dma(6)]
         + [dma(), dma(2), dma(2), dma(4), dma(4)]
         + [dma(1), dma(1), dma(depth), dma(depth), dma(3), dma(3)],
         compiler_params=pltpu.CompilerParams(
@@ -1616,9 +1620,31 @@
             sums[2] + jnp.sum(cot, axis=0, keepdims=True),
         )
 
+    seats = (place.s1, place.s2, place.s3)
+    part = width // 4
+    half = rows // 2
+
+    def go_copy(way, side):
+        src = datt_ref.at[pl.ds(side * half, half), aligned(seats[way] * part, part)]
+        dst = go_all.at[aligned(place.s * rows + side * half, half)]
+        return send(src, dst, (go_sent, go_got), 2 * way + side, place.across(way))
+
+    def go_arrival(way, side):
+        there = go_all.at[aligned(seats[way] * rows + side * half, half)]
+        return send(there, there, (go_sent, go_got), 2 * way + side, place.across(way))
+
     total.swap(0)
     none = jnp.zeros((1, width), F32)
-    gain_sum, bias_sum, cot_sum = over_rows(finish, (none, none, none))
+    sums = (none, none, none)
+    for side in (0, 1):
+        sums = lax.fori_loop(
+            0, lines // 2, lambda index, carry: finish(aligned(side * half + index * 32, 32), carry), sums
+        )
+        rows_here = pl.ds(side * half, half)
+        datt_ref[rows_here, :] = dot_nt(n2_sc[rows_here, :], out_w_ref[...]).astype(BF16)
+        for way in range(3):
+            go_copy(way, side).start()
+    gain_sum, bias_sum, cot_sum = sums
     small_ref[2:3, :] = gain_sum
     small_ref[3:4, :] = bias_sum
     small_ref[4:5, :] = cot_sum
@@ -1628,26 +1654,12 @@
     ]
     puts[0].start()
     puts[1].start()
-    if depth > 1:
-        total.close(depth - 1, False)
-    datt_ref[...] = dot_nt(n2_sc[...], out_w_ref[...]).astype(BF16)
-    seats = (place.s1, place.s2, place.s3)
-    part = width // 4
-
-    def go_copy(way):
-        src = datt_ref.at[:, aligned(seats[way] * part, part)]
-        return send(src, go_all.at[aligned(place.s * rows, rows)], (go_sent, go_got), way, place.across(way))
-
-    def go_arrival(way):
-        there = go_all.at[aligned(seats[way] * rows, rows)]
-        return send(there, there, (go_sent, go_got), way, place.across(way))
-
     own_go = pltpu.make_async_copy(
         datt_ref.at[:, aligned(place.s * part, part)], go_all.at[aligned(place.s * rows, rows)], go_sems
     )
-    for way in range(3):
-        go_copy(way).start()
     own_go.start()
+    if depth > 1:
+        total.close(depth - 1, False)
     out_g_ref[...] = dot_tn(att_ref[...], n2_sc[...]).astype(BF16)
     puts[2].start()
     total.close(0, True)
@@ -1659,8 +1671,9 @@
         put.wait()
     own_go.wait()
     for way in range(3):
-        go_arrival(way).wait_recv()
-        go_copy(way).wait_send()
+        for side in (0, 1):
+            go_arrival(way, side).wait_recv()
+            go_copy(way, side).wait_send()
     total.sent()
     place.each(1, depth, lambda step: total.z_copy(step).wait_send())
 
@@ -1699,8 +1712,8 @@
             dma(4),
             pltpu.VMEM((rows, width), BF16),
             dma(),
-            dma(3),
-            dma(3),
+            dma(6),
+            dma(6),
             pltpu.VMEM((rows, width), F32),
             pltpu.VMEM((rows, width), BF16),
             pltpu.VMEM((width, rows), BF16),

time: 278 us -> 275 us (0.989)
  Pallas kernels: 273 us -> 270 us
    pallas_call x1, Pallas kernels: 103 us -> 100 us  [backward_attention(): pl.pallas_call(functools.partial(backward_kernel, fsdp_count), out_shape=...]
where the time goes in v3:
time: 275 us
  Pallas kernels  270 us (98%)
    pallas_call x1, Pallas kernels, backward_attention(): pl.pallas_call(functools.partial(backward_kernel, fsdp_count), out_shape=...  100 us
    pallas_call x1, Pallas kernels, forward_attention(): pl.pallas_call(functools.partial(forward_kernel, fsdp_count), out_shape=(...  97 us
    pallas_call x1, Pallas kernels, middle(): pl.pallas_call(functools.partial(middle_kernel, fsdp_count), out_shape=(s...  67.1 us
    pallas_call x1, Pallas kernels, write_results(): pl.pallas_call(functools.partial(results_kernel, share, held), out_shape=...  5.95 us

profile of v3, /device:TPU:0, one launch (start us, length us, event | category | flops | bytes accessed | tf_op | source)
XLA Modules:
  0.0 274.7 jit_solution(10226680817511177174)
XLA Ops:
  0.6 0.0 copy-start
  0.7 0.1 pad.14.clone
  0.8 0.7 stack.23
  1.5 0.0 copy-done
  1.5 0.1 fusion.7
  1.6 0.1 fusion.5
  1.7 0.7 maximum_maximum_fusion.vec_ref
  2.4 0.8 copy.27
  3.2 0.2 fusion
  3.5 0.7 pad_maximum_fusion.mask_ref
  4.2 97.0 %shard_map.229 = (bf16[1536,768]{1,0:T(8,128)(2,1)}, f32[2,2,1536]{2,1,0:T(2,128)}, bf16[384,1024]{1,0:T(8,128)(2,1)}, bf16[1024,1024]{1,0:T(8,128)(2,1)}, bf16[...) custom-call(bf16[384,1024]{1,0:T(8,128)(2,1)} %bitcast.22, ...), custom_call_target="tpu_custom_call" | custom-call | tf_op jit(solution)/shard_map/pallas_call | solution.py:667
  101.2 67.1 %shard_map.230 = (bf16[384,1024]{1,0:T(8,128)(2,1)}, bf16[1536,256]{1,0:T(8,128)(2,1)}, f32[384,1024]{1,0:T(8,128)}, f32[16,1024]{1,0:T(8,128)}, bf16[1024,1024]...) custom-call(bf16[384,1024]{1,0:T(8,128)(2,1)} %get-tuple-element.48.att_hbm, ...), custom_call_target="tpu_custom_call" | custom-call | tf_op jit(solution)/shard_map/pallas_call | solution.py:1690
  168.3 100.3 %shard_map.231 = (bf16[384,1024]{1,0:T(8,128)(2,1)}, f32[16,1024]{1,0:T(8,128)}, bf16[128,3072]{1,0:T(8,128)(2,1)}, bf16[128,1024]{1,0:T(8,128)(2,1)}, bf16[128,...) custom-call(bf16[1536,256]{1,0:T(8,128)(2,1)} %get-tuple-element.53.go_hbm, bf16[1536,768]{1,0:T(8,128)(2,1)} %get-tuple-element.54.heads_hbm, ...), custom_call_target="tpu_custom_call" | custom-call | tf_op jit(solution)/shard_map/pallas_call | solution.py:1373
  268.6 6.0 %shard_map.232 = (f32[128,4096]{1,0:T(8,128)}, f32[512,1024]{1,0:T(8,128)}, f32[128,3072]{1,0:T(8,128)}, f32[128,1024]{1,0:T(8,128)}, bf16[384,1024]{1,0:T(8,128...) custom-call(bf16[128,4096]{1,0:T(8,128)(2,1)} %get-tuple-element.65., ...), custom_call_target="tpu_custom_call" | custom-call | tf_op jit(solution)/shard_map/pallas_call | solution.py:1792
  (11 shorter events, 0.1 us)
Async XLA Ops:
  0.6 0.9 copy-start

commit v4 on v3

--- a/solution.py
+++ b/solution.py
@@ -31,17 +31,21 @@
 DOCS = 6
 
 
-def block_mask(random_blocks):
-    heads, inner, _ = random_blocks.shape
-    blocks = inner + 2
-    ids = jnp.arange(blocks, dtype=jnp.int32)
-    near = jnp.abs(ids[:, None] - ids[None, :]) <= 1
-    edge = (ids == 0) | (ids == blocks - 1)
-    fixed = near | edge[:, None] | edge[None, :]
-    picked = jnp.any(random_blocks[:, :, :, None] == ids, axis=2)
-    used = fixed[None] | jnp.pad(picked, ((0, 0), (1, 1), (0, 0)))
-    row = jnp.pad(jnp.where(used, 0.0, NEG), ((0, 0), (0, 0), (0, DH - blocks)))
-    return jnp.concatenate([row, row], axis=-1)
+def write_block_mask(picks_ref, mask_ref):
+    heads, inner, count = picks_ref.shape
+    last = inner + 1
+    shape = (inner, LANES)
+    lane = lax.rem(lax.broadcasted_iota(jnp.int32, shape, 1), DH)
+    block = lax.broadcasted_iota(jnp.int32, shape, 0) + 1
+    fixed = (jnp.abs(lane - block) <= 1) | (lane == 0) | (lane >= last)
+    for head in range(heads):
+        picks = picks_ref[head]
+        used = fixed
+        for slot in range(count):
+            used = used | (picks[:, slot : slot + 1] == lane)
+        mask_ref[head, 0:1, :] = jnp.zeros((1, LANES), F32)
+        mask_ref[head, 1:last, :] = jnp.where(used, 0.0, NEG)
+        mask_ref[head, last : last + 1, :] = jnp.zeros((1, LANES), F32)
 
 
 def token_features(start, docs, blocks):
@@ -408,7 +412,7 @@
     wq_ref,
     vec_ref,
     ids_ref,
-    mask_ref,
+    picks_ref,
     out_w_ref,
     down_w_ref,
     in_w_ref,
@@ -423,6 +427,7 @@
     wq_all,
     qd_ref,
     kf_ref,
+    mask_ref,
     x_sc,
     n1_sc,
     wq_own,
@@ -468,6 +473,7 @@
     ]
     for pick in picks:
         pick.start()
+    write_block_mask(picks_ref, mask_ref)
     seg_ref[...] = jnp.zeros_like(seg_ref)
     for part in range(ids_ref.shape[1] // LANES):
         seg_ref[part : part + 1, :] = ids_ref[:, part * LANES : (part + 1) * LANES]
@@ -648,10 +654,10 @@
         one.finish()
 
 
-def forward_attention(fsdp_count, x, w_qkv, vec, seg, mask, w_out, w_down, w_in):
+def forward_attention(fsdp_count, x, w_qkv, vec, seg, picks, w_out, w_down, w_in):
     rows, width = x.shape
     length = 4 * rows
-    heads = mask.shape[0]
+    heads = picks.shape[0]
     pairs = heads // 2
     depth = fsdp_count // 2
     own_width = w_qkv.shape[1] // 4
@@ -678,9 +684,10 @@
             shape((full, own_width), BF16),
             shape((length, LANES), BF16),
             shape((length, LANES), BF16),
+            shape((heads, picks.shape[1] + 2, LANES), F32),
         ),
         in_specs=[anywhere] * 3 + [vmem] * 2 + [anywhere] * 3,
-        out_specs=(anywhere, vmem, anywhere, anywhere, anywhere, anywhere, vmem, anywhere, anywhere, vmem, vmem),
+        out_specs=(anywhere, vmem, anywhere, anywhere, anywhere, anywhere, vmem, anywhere, anywhere, vmem, vmem, vmem),
         scratch_shapes=[
             pltpu.VMEM((length, width), BF16),
             pltpu.VMEM((length, width), BF16),
@@ -701,7 +708,7 @@
         compiler_params=pltpu.CompilerParams(
             collective_id=2, has_side_effects=True, vmem_limit_bytes=60 << 20
         ),
-    )(x, w_qkv, vec, seg, mask, w_out, w_down, w_in)
+    )(x, w_qkv, vec, seg, picks, w_out, w_down, w_in)
 
 
 def by_rows(count, cols, body):
@@ -1835,9 +1842,8 @@
     broad = jnp.tile(b_in[None], (1, width // held))
     broad = jnp.where((line * width + column) // held == position, broad, jnp.zeros((), BF16))
     vec = jnp.concatenate([narrow, broad, jnp.zeros((-(5 + lines) % 16, width), BF16)], axis=0)
-    mask = block_mask(random_blocks)
-    by_heads, lse, att_rows, out_weight, down_weight, in_weight, vec, normed_one, own_qkv, query_docs, key_feats = (
-        forward_attention(fsdp_count, tokens[0], w_qkv, vec, segment_ids, mask, w_out, w_down, w_in)
+    by_heads, lse, att_rows, out_weight, down_weight, in_weight, vec, normed_one, own_qkv, query_docs, key_feats, mask = (
+        forward_attention(fsdp_count, tokens[0], w_qkv, vec, segment_ids, random_blocks, w_out, w_down, w_in)
     )
     result, grad_att, grad_hidden, small, grad_out, grad_in, down_part = middle(
         fsdp_count, att_rows, tokens[0], cotangent[0], vec, out_weight, in_weight, down_weight

time: 275 us -> 275 us (level)
  no operation moved by 1% of the time
where the time goes in v4:
time: 275 us
  Pallas kernels  271 us (99%)
    pallas_call x1, Pallas kernels, backward_attention(): pl.pallas_call(functools.partial(backward_kernel, fsdp_count), out_shape=...  100 us
    pallas_call x1, Pallas kernels, forward_attention(): pl.pallas_call(functools.partial(forward_kernel, fsdp_count), out_shape=(...  97.2 us
    pallas_call x1, Pallas kernels, middle(): pl.pallas_call(functools.partial(middle_kernel, fsdp_count), out_shape=(s...  67.1 us
    pallas_call x1, Pallas kernels, write_results(): pl.pallas_call(functools.partial(results_kernel, share, held), out_shape=...  5.95 us

profile of v4, /device:TPU:0, one launch (start us, length us, event | category | flops | bytes accessed | tf_op | source)
XLA Modules:
  0.0 274.5 jit_solution(9024429294638066670)
XLA Ops:
  0.6 0.0 copy-start
  0.7 0.1 pad.2.clone
  0.8 0.7 stack.23
  1.5 0.0 copy-done
  1.5 0.1 fusion.4
  1.7 0.7 maximum_maximum_fusion.vec_ref
  2.3 1.4 copy.26.picks_ref
  3.8 97.2 %shard_map.229 = (bf16[1536,768]{1,0:T(8,128)(2,1)}, f32[2,2,1536]{2,1,0:T(2,128)}, bf16[384,1024]{1,0:T(8,128)(2,1)}, bf16[1024,1024]{1,0:T(8,128)(2,1)}, bf16[...) custom-call(bf16[384,1024]{1,0:T(8,128)(2,1)} %bitcast.22, ...), custom_call_target="tpu_custom_call" | custom-call | tf_op jit(solution)/shard_map/pallas_call | solution.py:673
  101.0 67.1 %shard_map.230 = (bf16[384,1024]{1,0:T(8,128)(2,1)}, bf16[1536,256]{1,0:T(8,128)(2,1)}, f32[384,1024]{1,0:T(8,128)}, f32[16,1024]{1,0:T(8,128)}, bf16[1024,1024]...) custom-call(bf16[384,1024]{1,0:T(8,128)(2,1)} %get-tuple-element.49.att_hbm, ...), custom_call_target="tpu_custom_call" | custom-call | tf_op jit(solution)/shard_map/pallas_call | solution.py:1697
  168.1 100.3 %shard_map.231 = (bf16[384,1024]{1,0:T(8,128)(2,1)}, f32[16,1024]{1,0:T(8,128)}, bf16[128,3072]{1,0:T(8,128)(2,1)}, bf16[128,1024]{1,0:T(8,128)(2,1)}, bf16[128,...) custom-call(bf16[1536,256]{1,0:T(8,128)(2,1)} %get-tuple-element.54.go_hbm, bf16[1536,768]{1,0:T(8,128)(2,1)} %get-tuple-element.55.heads_hbm, ...), custom_call_target="tpu_custom_call" | custom-call | tf_op jit(solution)/shard_map/pallas_call | solution.py:1380
  268.4 6.0 %shard_map.232 = (f32[128,4096]{1,0:T(8,128)}, f32[512,1024]{1,0:T(8,128)}, f32[128,3072]{1,0:T(8,128)}, f32[128,1024]{1,0:T(8,128)}, bf16[384,1024]{1,0:T(8,128...) custom-call(bf16[128,4096]{1,0:T(8,128)(2,1)} %get-tuple-element.67., ...), custom_call_target="tpu_custom_call" | custom-call | tf_op jit(solution)/shard_map/pallas_call | solution.py:1799
  (7 shorter events, 0.0 us)
Async XLA Ops:
  0.6 0.9 copy-start

commit v5 on v4

--- a/solution.py
+++ b/solution.py
@@ -1585,9 +1585,9 @@
                 return carry
 
             lax.fori_loop(0, 2, early, 0)
+            total.fold(dest, None)
             swap_before(t)
             chunk(2 * t)
-            total.fold(dest, None)
             chunk(2 * t + 1)
             close_before(t)
             return carry

time: 275 us -> 273 us (level)
  Pallas kernels: 271 us -> 268 us
where the time goes in v5:
time: 273 us; the launch traced here: 272 us
  Pallas kernels  268 us (98%)
    pallas_call x1, Pallas kernels, backward_attention(): pl.pallas_call(functools.partial(backward_kernel, fsdp_count), out_shape=...  100 us
    pallas_call x1, Pallas kernels, forward_attention(): pl.pallas_call(functools.partial(forward_kernel, fsdp_count), out_shape=(...  97.2 us
    pallas_call x1, Pallas kernels, middle(): pl.pallas_call(functools.partial(middle_kernel, fsdp_count), out_shape=(s...  65.1 us
    pallas_call x1, Pallas kernels, write_results(): pl.pallas_call(functools.partial(results_kernel, share, held), out_shape=...  5.95 us

profile of v5, /device:TPU:0, one launch (start us, length us, event | category | flops | bytes accessed | tf_op | source)
XLA Modules:
  0.0 272.4 jit_solution(3436010070552396055)
XLA Ops:
  0.6 0.0 copy-start
  0.7 0.1 pad.2.clone
  0.8 0.7 stack.23
  1.5 0.0 copy-done
  1.5 0.1 fusion.4
  1.7 0.7 maximum_maximum_fusion.vec_ref
  2.3 1.4 copy.26.picks_ref
  3.8 97.2 %shard_map.229 = (bf16[1536,768]{1,0:T(8,128)(2,1)}, f32[2,2,1536]{2,1,0:T(2,128)}, bf16[384,1024]{1,0:T(8,128)(2,1)}, bf16[1024,1024]{1,0:T(8,128)(2,1)}, bf16[...) custom-call(bf16[384,1024]{1,0:T(8,128)(2,1)} %bitcast.22, ...), custom_call_target="tpu_custom_call" | custom-call | tf_op jit(solution)/shard_map/pallas_call | solution.py:673
  101.0 65.1 %shard_map.230 = (bf16[384,1024]{1,0:T(8,128)(2,1)}, bf16[1536,256]{1,0:T(8,128)(2,1)}, f32[384,1024]{1,0:T(8,128)}, f32[16,1024]{1,0:T(8,128)}, bf16[1024,1024]...) custom-call(bf16[384,1024]{1,0:T(8,128)(2,1)} %get-tuple-element.49.att_hbm, ...), custom_call_target="tpu_custom_call" | custom-call | tf_op jit(solution)/shard_map/pallas_call | solution.py:1697
  166.0 100.2 %shard_map.231 = (bf16[384,1024]{1,0:T(8,128)(2,1)}, f32[16,1024]{1,0:T(8,128)}, bf16[128,3072]{1,0:T(8,128)(2,1)}, bf16[128,1024]{1,0:T(8,128)(2,1)}, bf16[128,...) custom-call(bf16[1536,256]{1,0:T(8,128)(2,1)} %get-tuple-element.54.go_hbm, bf16[1536,768]{1,0:T(8,128)(2,1)} %get-tuple-element.55.heads_hbm, ...), custom_call_target="tpu_custom_call" | custom-call | tf_op jit(solution)/shard_map/pallas_call | solution.py:1380
  266.3 6.0 %shard_map.232 = (f32[128,4096]{1,0:T(8,128)}, f32[512,1024]{1,0:T(8,128)}, f32[128,3072]{1,0:T(8,128)}, f32[128,1024]{1,0:T(8,128)}, bf16[384,1024]{1,0:T(8,128...) custom-call(bf16[128,4096]{1,0:T(8,128)(2,1)} %get-tuple-element.67., ...), custom_call_target="tpu_custom_call" | custom-call | tf_op jit(solution)/shard_map/pallas_call | solution.py:1799
  (7 shorter events, 0.0 us)
Async XLA Ops:
  0.6 0.9 copy-start
